TPU v7x, 128 devices: a whole 4x4x4 slice. The times are simulated.
128 devices in a mesh: gx: 32 (over x, y, core), gy: 4 (over z).
Axes of the slice: x: 4, y: 4, z: 4, core: 2. Of those that a mesh axis runs over, the one named last changes fastest.
Arguments:
- fluid_state: float32 [512, 32, 768], P('gx', 'gy'), may hold values from -4 to 4, as said below
- cell_counts: int32 [512, 32], P('gx', 'gy'), may hold values from 24 to 64
- wall_blocks: float32 [32768, 512], P(('gx', 'gy')), may hold values from -2.5 to 4, as said below
- readers: int32 [32768, 2], P(('gx', 'gy')), may hold values from 0 to 127, all different within a row; in each aligned block of 256 rows (0 to 255, 256 to 511, ...) at most 8 rows name the same one
- targets: int32 [32768, 2], P(('gx', 'gy')), may hold values from 0 to 127
Outputs:
- fluid_rates: float32 [512, 32, 256], P('gx', 'gy')
- density_rate: float32 [512, 2048], P('gx', 'gy')
Inputs may be any that keep to these rules, and one draw needn't show every extreme that they name: The two readers of a wall block are different devices; among the wall blocks of one device at most 8 name the same reader. `fluid_state`: offsets x, y in [0, 1), depth in [0, 4), density in [0.97, 1.03], smoothing length in [0.3, 0.5], sound speed in [1, 2], mass in [0.04, 0.08], viscosity in [0.01, 0.04]. `wall_blocks`: wall positions x, y in [-0.2, 1.2], depth in [0, 4), Shepard correction in [0.5, 1].
All inputs are finite; a program needn't handle non-finite values.
Results may differ from a plain program's by a relative error of at most 0.0001.
Values sent between devices are 32-bit elements; how exact they have to be, the bound alone decides.
A program may use at most 64 MiB of HBM per device.

v0:
```python
import math

import jax
import jax.numpy as jnp
from jax import lax
from jax.sharding import PartitionSpec as P

KERN_W = 21.0 / (16.0 * math.pi)
KERN_F = 105.0 / (16.0 * math.pi)
KAPPA = 0.02
WALL_PUSH = 0.03
WALL_HEAT = 0.02
EPS_R = 0.01


def with_halo(array, sides, width):
    for axis, dim in sides:
        peers, length = (lax.axis_size(axis), array.shape[dim])
        up = [(i, (i + 1) % peers) for i in range(peers - 1)]
        down = [(j, i) for i, j in up]
        last = lax.slice_in_dim(array, length - width, length, axis=dim)
        first = lax.slice_in_dim(array, 0, width, axis=dim)
        before = lax.ppermute(last, axis, up)
        after = lax.ppermute(first, axis, down)
        array = jnp.concatenate([before, array, after], axis=dim)
    return array


def pair_records(fluid_state, cell_counts):
    comps = fluid_state.reshape(fluid_state.shape[:-1] + (12, 64))
    alive = (jnp.arange(64, dtype=jnp.int32) < cell_counts[..., None]).astype(fluid_state.dtype)
    density = comps[..., 7, :]
    inverse = 1.0 / density
    sound = comps[..., 9, :]
    pressure = sound * sound / 7.0 * (density**7 - 1.0)
    fields = [comps[..., k, :] for k in range(6)]
    fields = fields + [
        comps[..., 6, :] * alive,
        pressure * inverse * inverse,
        comps[..., 10, :] * inverse,
        inverse,
        comps[..., 8, :],
        comps[..., 11, :],
    ]
    return jnp.stack(fields, axis=-2).reshape(fluid_state.shape)


def pair_sums(center, neighbour, shift_x, shift_y):
    near = [center[..., k, :, None] for k in range(12)]
    far = [neighbour[..., k, None, :] for k in range(12)]
    delta_x = near[0] - far[0] - shift_x
    delta_y = near[1] - far[1] - shift_y
    delta_z = near[2] - far[2]
    dist_sq = delta_x * delta_x + delta_y * delta_y + delta_z * delta_z
    smooth = 0.5 * (near[10] + far[10])
    ratio = jnp.sqrt(dist_sq) / smooth
    shell = jnp.maximum(1.0 - 0.5 * ratio, 0.0)
    weighted = far[6] * -KERN_F * shell * shell * shell / smooth**5
    damping = dist_sq / (dist_sq + EPS_R * smooth * smooth)
    diff_u = near[3] - far[3]
    diff_v = near[4] - far[4]
    diff_w = near[5] - far[5]
    density_rate = jnp.sum(
        weighted * (diff_u * delta_x + diff_v * delta_y + diff_w * delta_z), axis=-1
    )
    pressure = near[7] + far[7]
    viscous = (near[8] * far[9] + far[8] * near[9]) * damping
    accel_x = jnp.sum(weighted * (viscous * diff_u - pressure * delta_x), axis=-1)
    accel_y = jnp.sum(weighted * (viscous * diff_v - pressure * delta_y), axis=-1)
    accel_z = jnp.sum(weighted * (viscous * diff_w - pressure * delta_z), axis=-1)
    heating = jnp.sum(
        weighted * (2.0 * KAPPA) * near[9] * far[9] * damping * (near[11] - far[11]), axis=-1
    )
    return jnp.stack([density_rate, accel_x, accel_y, accel_z, heating], axis=-2)


def neighbour_terms(center, extended):
    rows_a = center.shape[0]
    rows_b = center.shape[1]
    middle = center.reshape(rows_a, rows_b, 12, 64)
    totals = jnp.zeros((rows_a, rows_b, 5, 64), jnp.float32)
    for shift_x in (-1, 0, 1):
        for shift_y in (-1, 0, 1):
            beside = extended[
                1 + shift_x : 1 + shift_x + rows_a, 1 + shift_y : 1 + shift_y + rows_b
            ]
            totals = totals + pair_sums(
                middle, beside.reshape(rows_a, rows_b, 12, 64), float(shift_x), float(shift_y)
            )
    return totals


def wall_terms(cell_rows, wall_rows):
    count = cell_rows.shape[0]
    fluid_part = cell_rows.reshape(count, 12, 64)
    wall_part = wall_rows.reshape(count, 8, 64)
    delta_x = fluid_part[:, 0, :, None] - wall_part[:, 0, None, :]
    delta_y = fluid_part[:, 1, :, None] - wall_part[:, 1, None, :]
    delta_z = fluid_part[:, 2, :, None] - wall_part[:, 2, None, :]
    smooth = fluid_part[:, 8, :, None]
    ratio = jnp.sqrt(delta_x * delta_x + delta_y * delta_y + delta_z * delta_z) / smooth
    shell = jnp.maximum(1.0 - 0.5 * ratio, 0.0)
    kernel = KERN_W * shell**4 * (2.0 * ratio + 1.0) / (smooth * smooth * smooth)
    corrected = wall_part[:, 6, None, :] * kernel
    sound = fluid_part[:, 9, :]
    push = WALL_PUSH * sound * sound
    force_x = push * jnp.sum(corrected * wall_part[:, 3, None, :], axis=-1)
    force_y = push * jnp.sum(corrected * wall_part[:, 4, None, :], axis=-1)
    force_z = push * jnp.sum(corrected * wall_part[:, 5, None, :], axis=-1)
    heating = WALL_HEAT * jnp.sum(
        corrected * (wall_part[:, 7, None, :] - fluid_part[:, 11, :, None]), axis=-1
    )
    return jnp.stack([force_x, force_y, force_z, heating], axis=1).reshape(count, 256)


def finish(fluid_terms, wall_sum):
    rows_a = fluid_terms.shape[0]
    rows_b = fluid_terms.shape[1]
    walled = wall_sum.reshape(rows_a, rows_b, 4, 64)
    rates = (fluid_terms[:, :, 1:, :] + walled).reshape(rows_a, rows_b, 256)
    density = fluid_terms[:, :, 0, :].reshape(rows_a, rows_b * 64)
    return (rates, density)


def local(fluid_state, cell_counts, wall_blocks, readers, targets):
    cells_x = fluid_state.shape[0]
    cells_y = fluid_state.shape[1]
    width_x = lax.axis_size("gx")
    width_y = lax.axis_size("gy")
    devices = width_x * width_y
    wall_count = wall_blocks.shape[0]
    most = max(2, 4 * wall_count // devices)
    flat_fluid = fluid_state.reshape(cells_x * cells_y, 768)
    records = pair_records(fluid_state, cell_counts)
    extended = with_halo(records, (("gx", 0), ("gy", 1)), 1)
    destination = readers.reshape(-1)
    onehot = (destination[:, None] == jnp.arange(devices, dtype=jnp.int32)[None, :]).astype(
        jnp.int32
    )
    earlier = jnp.cumsum(onehot, axis=0) - onehot
    position = destination * most + jnp.sum(earlier * onehot, axis=1)
    copies = jnp.repeat(wall_blocks, readers.shape[1], axis=0)
    send_records = jnp.zeros((devices * most, 512), jnp.float32).at[position].set(copies)
    send_cells = (
        jnp.full((devices * most,), -1.0, jnp.float32)
        .at[position]
        .set(targets.reshape(-1).astype(jnp.float32))
    )
    wall_rows = lax.all_to_all(
        send_records.reshape(devices, most, 512),
        ("gx", "gy"),
        split_axis=0,
        concat_axis=0,
        tiled=True,
    )
    cell_ids = lax.all_to_all(
        send_cells.reshape(devices, most), ("gx", "gy"), split_axis=0, concat_axis=0, tiled=True
    )
    sources = cell_ids.shape[0]
    width = cell_ids.shape[1]
    alive = cell_ids >= 0.0
    chosen = jnp.where(alive, cell_ids, 0.0).astype(jnp.int32).reshape(-1)
    bundle = 16
    cell_rows = flat_fluid[chosen].reshape(sources // bundle, bundle * width, 768)
    grouped = wall_rows.reshape(sources // bundle, bundle * width, 512)
    contrib = lax.map(lambda pair_in: wall_terms(pair_in[0], pair_in[1]), (cell_rows, grouped))
    contrib = contrib.reshape(sources, width, 256) * alive[..., None].astype(jnp.float32)
    contrib, cell_ids = (contrib, cell_ids)
    fluid_terms = neighbour_terms(records, extended)
    landing = jnp.where(cell_ids >= 0.0, cell_ids, 0.0).astype(jnp.int32).reshape(-1)
    wall_sum = (
        jnp.zeros((cells_x * cells_y, 256), jnp.float32).at[landing].add(contrib.reshape(-1, 256))
    )
    rates, density = finish(fluid_terms, wall_sum)
    return (rates, density)


def solution(mesh):
    placed = (
        P("gx", "gy", None),
        P("gx", "gy"),
        P(("gx", "gy"), None),
        P(("gx", "gy"), None),
        P(("gx", "gy"), None),
    )
    return jax.shard_map(
        local,
        mesh=mesh,
        in_specs=placed,
        out_specs=(P("gx", "gy", None), P("gx", "gy")),
        check_vma=False,
    )
```

profile of v0, /device:TPU:99, one launch (start us, length us, event | category | flops | bytes accessed | tf_op | source)
XLA Modules:
  0.0 525.1 jit_solution(8002945390394912867)
XLA Ops:
  5.0 3.8 collective-permute-start
  9.4 1.9 collective-permute-start.1
  13.1 2.4 scatter_custom_fusion
  16.2 10.0 %all-to-all-start = ((f32[128,1,8]{2,1,0:T(1,128)}), f32[128,1,8]{2,1,0:T(1,128)S(1)}, u32[]{:S(2)}, u32[]{:S(2)}) async-start(f32[128,1,8]{2,1,0:T(1,128)} %bitcast.185), calls=%async_computation | async-start | bytes 131072 | tf_op jit(solution)/shard_map/all_to_all | solution.py:156
  26.3 21.4 %fusion.121 = (f32[16,8,64]{2,1,0:T(8,128)S(1)}, f32[16,8,64]{2,1,0:T(8,128)S(1)}, f32[16,8,64]{2,1,0:T(8,128)S(1)}, f32[16,8,64]{2,1,0:T(8,128)S(1)}, f32[16,8,64]{2,1,0:T(8,128)}) fusion(f32[16,8,64]{2,1,0:T(8,128)S(1)} %bitcast.660, f32[16,8,64]{2,1,0:T(8,128)S(1)} %bitcast.658, f32[16,8,64]{2,1,0:T(8,128)S(1)} %get-tuple-element.247, ...), kind=kLoop, calls=%fused_computation.285 | loop fusion | flops 31940608 | bytes 688128 | tf_op jit(solution)/shard_map/reduce_sum | solution.py:70
  49.9 3.7 scatter_custom_fusion.1
  53.6 10.1 %all-to-all-start.1 = ((f32[128,8,512]{2,1,0:T(8,128)}), f32[128,8,512]{2,1,0:T(8,128)S(1)}, u32[]{:S(2)}, u32[]{:S(2)}) async-start(f32[128,8,512]{2,1,0:T(8,128)} %bitcast.189), calls=%async_computation.1 | async-start | bytes 4194304 | tf_op jit(solution)/shard_map/all_to_all | solution.py:149
  65.4 5.3 %gather_fusion = f32[1024,768]{1,0:T(8,128)} fusion(f32[128,768]{1,0:T(8,128)S(1)} %bitcast.290, s32[1024]{0:T(1024)S(1)} %broadcast_clamp_fusion), kind=kCustom, calls=%fused_computation | custom fusion | bytes 6295552 | tf_op jit(solution)/shard_map/gather | solution.py:164
  70.7 1.3 constant_dynamic-update-slice_fusion.3
  72.0 2.3 pad_maximum_fusion.4
  74.3 2.2 reshape.260
  76.6 4.8 fusion.239
  81.4 11.5 %fusion.65 = f32[16,8,64]{2,1,0:T(8,128)S(1)} fusion(f32[16,8,64]{2,1,0:T(8,128)S(1)} %bitcast.631, f32[16,8,64]{2,1,0:T(8,128)S(1)} %bitcast.629, f32[16,8,64]{2,1,0:T(8,128)S(1)} %bitcast.477, f32[16,8,64]{2,1,0:T(8,128)S(1)} %bitcast.611, f32[16,8,64]{2,1,0:T(8,128)S(1)} %bitcast.489, f32[16,8,64]{2,1,0:T(8,128)S(1)} %get-tuple-element.253, ...), kind=kLoop, calls=%fused_computation.229 | loop fusion | flops 19390464 | bytes 589824 | tf_op jit(solution)/shard_map/reduce_sum | solution.py:68
  92.9 14.0 %fusion.71 = (f32[16,8,64]{2,1,0:T(8,128)S(1)}, f32[16,8,64]{2,1,0:T(8,128)S(1)}) fusion(f32[16,8,64]{2,1,0:T(8,128)S(1)} %bitcast.632, f32[16,8,64]{2,1,0:T(8,128)S(1)} %bitcast.630, f32[16,8,64]{2,1,0:T(8,128)S(1)} %bitcast.478, f32[16,8,64]{2,1,0:T(8,128)S(1)} %bitcast.665, f32[16,8,64]{2,1,0:T(8,128)S(1)} %bitcast.484, ...), kind=kLoop, calls=%fused_computation.235 | loop fusion | flops 22528000 | bytes 688128 | tf_op jit(solution)/shard_map/reduce_sum | solution.py:70
  107.0 14.4 %multiply_reduce_fusion.11 = (f32[16,8,64]{2,1,0:T(8,128)}, f32[16,8,64]{2,1,0:T(8,128)S(1)}) fusion(f32[16,8,64]{2,1,0:T(8,128)S(1)} %bitcast.695, f32[16,8,64]{2,1,0:T(8,128)S(1)} %bitcast.479, f32[16,8,64]{2,1,0:T(8,128)S(1)} %bitcast.448, f32[16,8,64]{2,1,0:T(8,128)S(1)} %get-tuple-element.252, f32[16,8,64]{2,1,0:T(8,128)S(1)} %bitcast.482, ...), kind=kLoop, calls=%fused_computation.400 | loop fusion | flops 22003712 | bytes 688128 | tf_op jit(solution)/shard_map/reduce_sum | solution.py:71
  122.0 1.3 constant_dynamic-update-slice_fusion.1
  123.3 1.8 fusion.249
  125.2 1.3 collective-permute-start.2
  126.5 4.6 collective-permute-start.3
  132.4 4.8 fusion.245
  137.2 11.5 %fusion.169 = f32[16,8,64]{2,1,0:T(8,128)S(1)} fusion(f32[16,8,64]{2,1,0:T(8,128)S(1)} %bitcast.635, f32[16,8,64]{2,1,0:T(8,128)S(1)} %bitcast.633, f32[16,8,64]{2,1,0:T(8,128)S(1)} %bitcast.495, f32[16,8,64]{2,1,0:T(8,128)S(1)} %bitcast.613, f32[16,8,64]{2,1,0:T(8,128)S(1)} %bitcast.507, f32[16,8,64]{2,1,0:T(8,128)S(1)} %get-tuple-element.253, ...), kind=kLoop, calls=%fused_computation.333 | loop fusion | flops 19390464 | bytes 589824 | tf_op jit(solution)/shard_map/reduce_sum | solution.py:68
  148.7 14.0 %fusion.175 = (f32[16,8,64]{2,1,0:T(8,128)S(1)}, f32[16,8,64]{2,1,0:T(8,128)S(1)}) fusion(f32[16,8,64]{2,1,0:T(8,128)S(1)} %bitcast.636, f32[16,8,64]{2,1,0:T(8,128)S(1)} %bitcast.634, f32[16,8,64]{2,1,0:T(8,128)S(1)} %bitcast.496, f32[16,8,64]{2,1,0:T(8,128)S(1)} %bitcast.669, f32[16,8,64]{2,1,0:T(8,128)S(1)} %bitcast.502, ...), kind=kLoop, calls=%fused_computation.339 | loop fusion | flops 22528000 | bytes 688128 | tf_op jit(solution)/shard_map/reduce_sum | solution.py:70
  162.7 14.4 %multiply_reduce_fusion.5 = (f32[16,8,64]{2,1,0:T(8,128)}, f32[16,8,64]{2,1,0:T(8,128)S(1)}) fusion(f32[16,8,64]{2,1,0:T(8,128)S(1)} %bitcast.696, f32[16,8,64]{2,1,0:T(8,128)S(1)} %bitcast.497, f32[16,8,64]{2,1,0:T(8,128)S(1)} %bitcast.449, f32[16,8,64]{2,1,0:T(8,128)S(1)} %get-tuple-element.252, f32[16,8,64]{2,1,0:T(8,128)S(1)} %bitcast.500, ...), kind=kLoop, calls=%fused_computation.381 | loop fusion | flops 22003712 | bytes 688128 | tf_op jit(solution)/shard_map/reduce_sum | solution.py:71
  179.8 3.7 fusion.218
  183.4 2.2 reshape.259
  185.7 4.8 fusion.240
  190.5 11.6 %fusion.47 = f32[16,8,64]{2,1,0:T(8,128)S(1)} fusion(f32[16,8,64]{2,1,0:T(8,128)S(1)} %bitcast.639, f32[16,8,64]{2,1,0:T(8,128)S(1)} %get-tuple-element.253, f32[16,8,64]{2,1,0:T(8,128)S(1)} %get-tuple-element.254, f32[16,8,64]{2,1,0:T(8,128)S(1)} %bitcast.637, f32[16,8,64]{2,1,0:T(8,128)S(1)} %bitcast.513, f32[16,8,64]{2,1,0:T(8,128)S(1)} %get-tuple-element.251, ...), kind=kLoop, calls=%fused_computation.211 | loop fusion | flops 19914752 | bytes 589824 | tf_op jit(solution)/shard_map/reduce_sum | solution.py:68
  202.2 14.7 %fusion.53 = (f32[16,8,64]{2,1,0:T(8,128)}, f32[16,8,64]{2,1,0:T(8,128)}) fusion(f32[16,8,64]{2,1,0:T(8,128)S(1)} %bitcast.640, f32[16,8,64]{2,1,0:T(8,128)S(1)} %get-tuple-element.253, f32[16,8,64]{2,1,0:T(8,128)S(1)} %get-tuple-element.254, f32[16,8,64]{2,1,0:T(8,128)S(1)} %bitcast.638, f32[16,8,64]{2,1,0:T(8,128)S(1)} %bitcast.514, ...), kind=kLoop, calls=%fused_computation.217 | loop fusion | flops 23052288 | bytes 688128 | tf_op jit(solution)/shard_map/reduce_sum | solution.py:70
  216.9 14.6 %multiply_reduce_fusion.12 = (f32[16,8,64]{2,1,0:T(8,128)}, f32[16,8,64]{2,1,0:T(8,128)S(1)}) fusion(f32[16,8,64]{2,1,0:T(8,128)S(1)} %bitcast.697, f32[16,8,64]{2,1,0:T(8,128)S(1)} %bitcast.450, f32[16,8,64]{2,1,0:T(8,128)S(1)} %get-tuple-element.252, f32[16,8,64]{2,1,0:T(8,128)S(1)} %bitcast.515, f32[16,8,64]{2,1,0:T(8,128)S(1)} %bitcast.518, ...), kind=kLoop, calls=%fused_computation.403 | loop fusion | flops 22528000 | bytes 688128 | tf_op jit(solution)/shard_map/reduce_sum | solution.py:71
  232.2 2.2 reshape.262
  234.4 4.8 fusion.242
  239.3 11.6 %fusion.97 = f32[16,8,64]{2,1,0:T(8,128)S(1)} fusion(f32[16,8,64]{2,1,0:T(8,128)S(1)} %bitcast.643, f32[16,8,64]{2,1,0:T(8,128)S(1)} %bitcast.641, f32[16,8,64]{2,1,0:T(8,128)S(1)} %bitcast.531, f32[16,8,64]{2,1,0:T(8,128)S(1)} %bitcast.617, f32[16,8,64]{2,1,0:T(8,128)S(1)} %bitcast.543, f32[16,8,64]{2,1,0:T(8,128)S(1)} %get-tuple-element.253, ...), kind=kLoop, calls=%fused_computation.261 | loop fusion | flops 19390464 | bytes 589824 | tf_op jit(solution)/shard_map/reduce_sum | solution.py:68
  250.9 14.6 %fusion.107 = (f32[16,8,64]{2,1,0:T(8,128)}, f32[16,8,64]{2,1,0:T(8,128)}) fusion(f32[16,8,64]{2,1,0:T(8,128)S(1)} %bitcast.644, f32[16,8,64]{2,1,0:T(8,128)S(1)} %bitcast.642, f32[16,8,64]{2,1,0:T(8,128)S(1)} %bitcast.532, f32[16,8,64]{2,1,0:T(8,128)S(1)} %bitcast.677, f32[16,8,64]{2,1,0:T(8,128)S(1)} %bitcast.538, ...), kind=kLoop, calls=%fused_computation.271 | loop fusion | flops 22528000 | bytes 688128 | tf_op jit(solution)/shard_map/reduce_sum | solution.py:70
  265.5 14.7 %multiply_reduce_fusion.9 = (f32[16,8,64]{2,1,0:T(8,128)}, f32[16,8,64]{2,1,0:T(8,128)S(1)}) fusion(f32[16,8,64]{2,1,0:T(8,128)S(1)} %bitcast.698, f32[16,8,64]{2,1,0:T(8,128)S(1)} %bitcast.533, f32[16,8,64]{2,1,0:T(8,128)S(1)} %bitcast.451, f32[16,8,64]{2,1,0:T(8,128)S(1)} %get-tuple-element.252, f32[16,8,64]{2,1,0:T(8,128)S(1)} %bitcast.536, ...), kind=kLoop, calls=%fused_computation.393 | loop fusion | flops 22003712 | bytes 688128 | tf_op jit(solution)/shard_map/reduce_sum | solution.py:71
  280.8 2.2 reshape.261
  283.1 4.8 fusion.241
  287.9 12.0 %fusion.83 = f32[16,8,64]{2,1,0:T(8,128)S(1)} fusion(f32[16,8,64]{2,1,0:T(8,128)S(1)} %bitcast.647, f32[16,8,64]{2,1,0:T(8,128)S(1)} %bitcast.645, f32[16,8,64]{2,1,0:T(8,128)S(1)} %bitcast.549, f32[16,8,64]{2,1,0:T(8,128)S(1)} %bitcast.619, f32[16,8,64]{2,1,0:T(8,128)S(1)} %bitcast.561, f32[16,8,64]{2,1,0:T(8,128)S(1)} %get-tuple-element.253, ...), kind=kLoop, calls=%fused_computation.247 | loop fusion | flops 19914752 | bytes 589824 | tf_op jit(solution)/shard_map/reduce_sum | solution.py:68
  300.0 14.7 %fusion.89 = (f32[16,8,64]{2,1,0:T(8,128)}, f32[16,8,64]{2,1,0:T(8,128)}) fusion(f32[16,8,64]{2,1,0:T(8,128)S(1)} %bitcast.648, f32[16,8,64]{2,1,0:T(8,128)S(1)} %bitcast.646, f32[16,8,64]{2,1,0:T(8,128)S(1)} %bitcast.550, f32[16,8,64]{2,1,0:T(8,128)S(1)} %bitcast.681, f32[16,8,64]{2,1,0:T(8,128)S(1)} %bitcast.556, f32[16,8,64]{2,1,0:T(8,128)S(1)} %get-tuple-element.253, ...), kind=kLoop, calls=%fused_computation.253 | loop fusion | flops 23052288 | bytes 688128 | tf_op jit(solution)/shard_map/reduce_sum | solution.py:70
  314.7 14.6 %multiply_reduce_fusion.10 = (f32[16,8,64]{2,1,0:T(8,128)}, f32[16,8,64]{2,1,0:T(8,128)S(1)}) fusion(f32[16,8,64]{2,1,0:T(8,128)S(1)} %bitcast.699, f32[16,8,64]{2,1,0:T(8,128)S(1)} %bitcast.551, f32[16,8,64]{2,1,0:T(8,128)S(1)} %bitcast.452, f32[16,8,64]{2,1,0:T(8,128)S(1)} %get-tuple-element.252, f32[16,8,64]{2,1,0:T(8,128)S(1)} %bitcast.554, ...), kind=kLoop, calls=%fused_computation.396 | loop fusion | flops 22528000 | bytes 688128 | tf_op jit(solution)/shard_map/reduce_sum | solution.py:71
  329.9 2.2 reshape.263
  332.2 4.8 fusion.243
  337.0 11.6 %fusion.129 = f32[16,8,64]{2,1,0:T(8,128)S(1)} fusion(f32[16,8,64]{2,1,0:T(8,128)S(1)} %bitcast.651, f32[16,8,64]{2,1,0:T(8,128)S(1)} %bitcast.649, f32[16,8,64]{2,1,0:T(8,128)S(1)} %bitcast.567, f32[16,8,64]{2,1,0:T(8,128)S(1)} %bitcast.621, f32[16,8,64]{2,1,0:T(8,128)S(1)} %bitcast.579, f32[16,8,64]{2,1,0:T(8,128)S(1)} %get-tuple-element.253, ...), kind=kLoop, calls=%fused_computation.293 | loop fusion | flops 19390464 | bytes 589824 | tf_op jit(solution)/shard_map/reduce_sum | solution.py:68
  348.7 14.6 %fusion.139 = (f32[16,8,64]{2,1,0:T(8,128)}, f32[16,8,64]{2,1,0:T(8,128)}) fusion(f32[16,8,64]{2,1,0:T(8,128)S(1)} %bitcast.652, f32[16,8,64]{2,1,0:T(8,128)S(1)} %bitcast.650, f32[16,8,64]{2,1,0:T(8,128)S(1)} %bitcast.568, f32[16,8,64]{2,1,0:T(8,128)S(1)} %bitcast.685, f32[16,8,64]{2,1,0:T(8,128)S(1)} %bitcast.574, ...), kind=kLoop, calls=%fused_computation.303 | loop fusion | flops 22528000 | bytes 688128 | tf_op jit(solution)/shard_map/reduce_sum | solution.py:70
  363.3 14.7 %multiply_reduce_fusion.7 = (f32[16,8,64]{2,1,0:T(8,128)}, f32[16,8,64]{2,1,0:T(8,128)S(1)}) fusion(f32[16,8,64]{2,1,0:T(8,128)S(1)} %bitcast.700, f32[16,8,64]{2,1,0:T(8,128)S(1)} %bitcast.569, f32[16,8,64]{2,1,0:T(8,128)S(1)} %bitcast.453, f32[16,8,64]{2,1,0:T(8,128)S(1)} %get-tuple-element.252, f32[16,8,64]{2,1,0:T(8,128)S(1)} %bitcast.572, ...), kind=kLoop, calls=%fused_computation.388 | loop fusion | flops 22003712 | bytes 688128 | tf_op jit(solution)/shard_map/reduce_sum | solution.py:71
  378.6 2.2 reshape.264
  380.9 4.8 fusion.244
  385.7 12.2 %fusion.151 = f32[16,8,64]{2,1,0:T(8,128)} fusion(f32[16,8,64]{2,1,0:T(8,128)S(1)} %bitcast.655, f32[16,8,64]{2,1,0:T(8,128)S(1)} %bitcast.653, f32[16,8,64]{2,1,0:T(8,128)S(1)} %bitcast.585, f32[16,8,64]{2,1,0:T(8,128)S(1)} %bitcast.623, f32[16,8,64]{2,1,0:T(8,128)S(1)} %bitcast.597, f32[16,8,64]{2,1,0:T(8,128)S(1)} %get-tuple-element.253, ...), kind=kLoop, calls=%fused_computation.315 | loop fusion | flops 19914752 | bytes 589824 | tf_op jit(solution)/shard_map/reduce_sum | solution.py:68
  397.9 14.7 %fusion.157 = (f32[16,8,64]{2,1,0:T(8,128)}, f32[16,8,64]{2,1,0:T(8,128)}) fusion(f32[16,8,64]{2,1,0:T(8,128)S(1)} %bitcast.656, f32[16,8,64]{2,1,0:T(8,128)S(1)} %bitcast.654, f32[16,8,64]{2,1,0:T(8,128)S(1)} %bitcast.586, f32[16,8,64]{2,1,0:T(8,128)S(1)} %bitcast.689, f32[16,8,64]{2,1,0:T(8,128)S(1)} %bitcast.592, ...), kind=kLoop, calls=%fused_computation.321 | loop fusion | flops 23052288 | bytes 688128 | tf_op jit(solution)/shard_map/reduce_sum | solution.py:70
  412.6 14.6 %multiply_reduce_fusion.6 = (f32[16,8,64]{2,1,0:T(8,128)}, f32[16,8,64]{2,1,0:T(8,128)S(1)}) fusion(f32[16,8,64]{2,1,0:T(8,128)S(1)} %bitcast.701, f32[16,8,64]{2,1,0:T(8,128)S(1)} %bitcast.587, f32[16,8,64]{2,1,0:T(8,128)S(1)} %bitcast.454, f32[16,8,64]{2,1,0:T(8,128)S(1)} %get-tuple-element.252, f32[16,8,64]{2,1,0:T(8,128)S(1)} %bitcast.590, ...), kind=kLoop, calls=%fused_computation.384 | loop fusion | flops 22528000 | bytes 688128 | tf_op jit(solution)/shard_map/reduce_sum | solution.py:71
  429.2 4.8 fusion.246
  434.2 11.6 %fusion.187 = f32[16,8,64]{2,1,0:T(8,128)S(1)} fusion(f32[16,8,64]{2,1,0:T(8,128)S(1)} %bitcast.627, f32[16,8,64]{2,1,0:T(8,128)S(1)} %bitcast.625, f32[16,8,64]{2,1,0:T(8,128)S(1)} %bitcast.459, f32[16,8,64]{2,1,0:T(8,128)S(1)} %bitcast.609, f32[16,8,64]{2,1,0:T(8,128)S(1)} %bitcast.471, f32[16,8,64]{2,1,0:T(8,128)S(1)} %get-tuple-element.253, ...), kind=kLoop, calls=%fused_computation.351 | loop fusion | flops 19914752 | bytes 589824 | tf_op jit(solution)/shard_map/reduce_sum | solution.py:68
  445.9 14.2 %fusion.193 = (f32[16,8,64]{2,1,0:T(8,128)S(1)}, f32[16,8,64]{2,1,0:T(8,128)S(1)}) fusion(f32[16,8,64]{2,1,0:T(8,128)S(1)} %bitcast.628, f32[16,8,64]{2,1,0:T(8,128)S(1)} %bitcast.626, f32[16,8,64]{2,1,0:T(8,128)S(1)} %bitcast.460, f32[16,8,64]{2,1,0:T(8,128)S(1)} %bitcast.661, f32[16,8,64]{2,1,0:T(8,128)S(1)} %bitcast.466, ...), kind=kLoop, calls=%fused_computation.357 | loop fusion | flops 23052288 | bytes 688128 | tf_op jit(solution)/shard_map/reduce_sum | solution.py:70
  460.1 14.0 %multiply_reduce_fusion.4 = (f32[16,8,64]{2,1,0:T(8,128)S(1)}, f32[16,8,64]{2,1,0:T(8,128)S(1)}) fusion(f32[16,8,64]{2,1,0:T(8,128)S(1)} %bitcast.694, f32[16,8,64]{2,1,0:T(8,128)S(1)} %bitcast.461, f32[16,8,64]{2,1,0:T(8,128)S(1)} %bitcast.455, f32[16,8,64]{2,1,0:T(8,128)S(1)} %get-tuple-element.252, f32[16,8,64]{2,1,0:T(8,128)S(1)} %bitcast.464, ...), kind=kLoop, calls=%fused_computation.377 | loop fusion | flops 22528000 | bytes 688128 | tf_op jit(solution)/shard_map/reduce_sum | solution.py:71
  475.7 40.5 %while.10 = (s32[]{:T(128)}, f32[8,128,256]{2,1,0:T(8,128)}, f32[8,128,768]{2,1,0:T(8,128)}, f32[8,128,512]{2,1,0:T(8,128)S(1)}, s32[]{:T(128)}) while((s32[]{:T(128)}, f32[8,128,256]{2,1,0:T(8,128)}, f32[8,128,768]{2,1,0:T(8,128)}, f32[8,128,512]{2,1,0:T(8,128)S(1)}, s32[]{:T(128)}) %tuple.203), condition=%wide.region_55.56_spmd, body=%wide.region_50.55_spmd.sunk | while | flops 15335426 | bytes 5210693 | solution.py:166
  477.1 2.8 multiply_reduce_fusion.14
  482.1 2.8 multiply_reduce_fusion.14
  487.2 2.8 multiply_reduce_fusion.14
  492.3 2.8 multiply_reduce_fusion.14
  497.3 2.8 multiply_reduce_fusion.14
  502.4 2.8 multiply_reduce_fusion.14
  507.4 2.8 multiply_reduce_fusion.14
  512.5 2.8 multiply_reduce_fusion.14
  516.2 1.4 bitcast_multiply_fusion.3
  517.6 6.1 %scatter_custom_fusion.2 = f32[128,256]{1,0:T(8,128)S(1)} fusion(s32[1024]{0:T(1024)S(1)} %bitcast.705, f32[1024,256]{1,0:T(8,128)S(1)} %bitcast_multiply_fusion.3, f32[]{:T(128)} %constant.75.clone.1), kind=kCustom, calls=%fused_computation.508 | custom fusion | flops 262144 | bytes 131076 | tf_op jit(solution)/shard_map/scatter-add | solution.py:172
  (250 shorter events, 39.9 us)
Async XLA Ops:
  1.9 9.5 %copy-start.31 = (s32[256,2]{0,1:T(2,128)S(1)}, s32[256,2]{0,1:T(2,128)}, u32[]{:S(2)}) copy-start(s32[256,2]{0,1:T(2,128)} %param.10) | copy-start | bytes 6148
  2.7 9.8 %copy-start.32 = (s32[256,2]{0,1:T(2,128)S(1)}, s32[256,2]{0,1:T(2,128)}, u32[]{:S(2)}) copy-start(s32[256,2]{0,1:T(2,128)} %param.11) | copy-start | bytes 6148
  5.0 65.7 %collective-permute-start = (f32[1,8,768]{2,1,0:T(8,128)}, f32[1,8,768]{2,1,0:T(8,128)}, u32[]{:S(2)}, u32[]{:S(2)}) collective-permute-start(f32[1,8,768]{2,1,0:T(8,128)} %slice.439), channel_id=1, source_target_pairs={{0,4},{4,8},{8,12},{12,16},{16,20},{20,24},{24,28},{28,32},{32,36}... | collective-permute-start | bytes 73736 | tf_op jit(solution)/shard_map/ppermute | solution.py:23
  9.4 62.6 %collective-permute-start.1 = (f32[1,8,768]{2,1,0:T(8,128)}, f32[1,8,768]{2,1,0:T(8,128)}, u32[]{:S(2)}, u32[]{:S(2)}) collective-permute-start(f32[1,8,768]{2,1,0:T(8,128)} %slice.441), channel_id=1, source_target_pairs={{4,0},{8,4},{12,8},{16,12},{20,16},{24,20},{28,24},{32,28},{36,32}... | collective-permute-start | bytes 73736 | tf_op jit(solution)/shard_map/ppermute | solution.py:24
  12.2 36.6 %copy-start.1 = (f32[256,512]{1,0:T(8,128)S(1)}, f32[256,512]{1,0:T(8,128)}, u32[]{:S(2)}) copy-start(f32[256,512]{1,0:T(8,128)} %param.9) | copy-start | bytes 1572868
  16.2 37.4 %all-to-all-start = ((f32[128,1,8]{2,1,0:T(1,128)}), f32[128,1,8]{2,1,0:T(1,128)S(1)}, u32[]{:S(2)}, u32[]{:S(2)}) async-start(f32[128,1,8]{2,1,0:T(1,128)} %bitcast.185), calls=%async_computation | async-start | bytes 131072 | tf_op jit(solution)/shard_map/all_to_all | solution.py:156
  47.7 1.1 copy-start.10
  49.9 15.5 %copy-start = (f32[16,8,768]{2,1,0:T(8,128)S(1)}, f32[16,8,768]{2,1,0:T(8,128)}, u32[]{:S(2)}) copy-start(f32[16,8,768]{2,1,0:T(8,128)} %param.7) | copy-start | bytes 1179652
  53.6 422.1 %all-to-all-start.1 = ((f32[128,8,512]{2,1,0:T(8,128)}), f32[128,8,512]{2,1,0:T(8,128)S(1)}, u32[]{:S(2)}, u32[]{:S(2)}) async-start(f32[128,8,512]{2,1,0:T(8,128)} %bitcast.189), calls=%async_computation.1 | async-start | bytes 4194304 | tf_op jit(solution)/shard_map/all_to_all | solution.py:149
  125.2 53.9 %collective-permute-start.2 = (f32[18,1,768]{2,1,0:T(1,128)}, f32[18,1,768]{2,1,0:T(1,128)}, u32[]{:S(2)}, u32[]{:S(2)}) collective-permute-start(f32[18,1,768]{2,1,0:T(1,128)} %get-tuple-element.242), channel_id=1, source_target_pairs={{0,1},{1,2},{2,3},{4,5},{5,6},{6,7},{8,9},{9,10},{10,11},{12,13},{... | collective-permute-start | bytes 165896 | tf_op jit(solution)/shard_map/ppermute | solution.py:23
  126.5 53.3 %collective-permute-start.3 = (f32[18,1,768]{2,1,0:T(1,128)S(1)}, f32[18,1,768]{2,1,0:T(1,128)}, u32[]{:S(2)}, u32[]{:S(2)}) collective-permute-start(f32[18,1,768]{2,1,0:T(1,128)S(1)} %get-tuple-element.243), channel_id=1, source_target_pairs={{1,0},{2,1},{3,2},{5,4},{6,5},{7,6},{9,8},{10,9},{11,10},{13,12},{... | collective-permute-start | bytes 165896 | tf_op jit(solution)/shard_map/ppermute | solution.py:24
  179.0 0.7 copy-start.8
  429.2 45.0 %copy-start.2 = (f32[16,8,5,64]{3,1,0,2:T(8,128)S(1)}, f32[16,8,5,64]{3,1,0,2:T(8,128)}, u32[]{:S(2)}) copy-start(f32[16,8,5,64]{3,1,0,2:T(8,128)} %constant_dynamic-update-slice_fusion.8) | copy-start | bytes 491524
  429.2 45.0 %copy-start.14 = (f32[16,8,64]{2,1,0:T(8,128)S(1)}, f32[16,8,64]{2,1,0:T(8,128)}, u32[]{:S(2)}) copy-start(f32[16,8,64]{2,1,0:T(8,128)} %get-tuple-element.52) | copy-start | bytes 98308
  429.2 45.0 %copy-start.13 = (f32[16,8,64]{2,1,0:T(8,128)S(1)}, f32[16,8,64]{2,1,0:T(8,128)}, u32[]{:S(2)}) copy-start(f32[16,8,64]{2,1,0:T(8,128)} %get-tuple-element.51) | copy-start | bytes 98308
  429.2 45.0 %copy-start.3 = (f32[16,8,5,64]{3,1,0,2:T(8,128)S(1)}, f32[16,8,5,64]{3,1,0,2:T(8,128)}, u32[]{:S(2)}) copy-start(f32[16,8,5,64]{3,1,0,2:T(8,128)} %constant_dynamic-update-slice_fusion.23) | copy-start | bytes 491524
  429.2 45.1 %copy-start.16 = (f32[16,8,64]{2,1,0:T(8,128)S(1)}, f32[16,8,64]{2,1,0:T(8,128)}, u32[]{:S(2)}) copy-start(f32[16,8,64]{2,1,0:T(8,128)} %get-tuple-element.56) | copy-start | bytes 98308
  429.2 45.1 %copy-start.15 = (f32[16,8,64]{2,1,0:T(8,128)S(1)}, f32[16,8,64]{2,1,0:T(8,128)}, u32[]{:S(2)}) copy-start(f32[16,8,64]{2,1,0:T(8,128)} %get-tuple-element.55) | copy-start | bytes 98308
  429.2 45.1 %copy-start.4 = (f32[16,8,5,64]{3,1,0,2:T(8,128)S(1)}, f32[16,8,5,64]{3,1,0,2:T(8,128)}, u32[]{:S(2)}) copy-start(f32[16,8,5,64]{3,1,0,2:T(8,128)} %constant_dynamic-update-slice_fusion.18) | copy-start | bytes 491524
  429.2 45.1 %copy-start.18 = (f32[16,8,64]{2,1,0:T(8,128)S(1)}, f32[16,8,64]{2,1,0:T(8,128)}, u32[]{:S(2)}) copy-start(f32[16,8,64]{2,1,0:T(8,128)} %get-tuple-element.54) | copy-start | bytes 98308
  429.2 45.1 %copy-start.17 = (f32[16,8,64]{2,1,0:T(8,128)S(1)}, f32[16,8,64]{2,1,0:T(8,128)}, u32[]{:S(2)}) copy-start(f32[16,8,64]{2,1,0:T(8,128)} %get-tuple-element.53) | copy-start | bytes 98308
  429.2 45.1 %copy-start.5 = (f32[16,8,5,64]{3,1,0,2:T(8,128)S(1)}, f32[16,8,5,64]{3,1,0,2:T(8,128)}, u32[]{:S(2)}) copy-start(f32[16,8,5,64]{3,1,0,2:T(8,128)} %constant_dynamic-update-slice_fusion.33) | copy-start | bytes 491524
  429.2 45.2 %copy-start.20 = (f32[16,8,64]{2,1,0:T(8,128)S(1)}, f32[16,8,64]{2,1,0:T(8,128)}, u32[]{:S(2)}) copy-start(f32[16,8,64]{2,1,0:T(8,128)} %get-tuple-element.58) | copy-start | bytes 98308
  434.1 40.4 %copy-start.19 = (f32[16,8,64]{2,1,0:T(8,128)S(1)}, f32[16,8,64]{2,1,0:T(8,128)}, u32[]{:S(2)}) copy-start(f32[16,8,64]{2,1,0:T(8,128)} %get-tuple-element.57) | copy-start | bytes 98308
  434.1 40.4 %copy-start.6 = (f32[16,8,5,64]{3,1,0,2:T(8,128)S(1)}, f32[16,8,5,64]{3,1,0,2:T(8,128)}, u32[]{:S(2)}) copy-start(f32[16,8,5,64]{3,1,0,2:T(8,128)} %constant_dynamic-update-slice_fusion.38) | copy-start | bytes 491524
  434.1 40.4 %copy-start.12 = (f32[16,8,64]{2,1,0:T(8,128)S(1)}, f32[16,8,64]{2,1,0:T(8,128)}, u32[]{:S(2)}) copy-start(f32[16,8,64]{2,1,0:T(8,128)} %fusion.151) | copy-start | bytes 98308
  434.1 40.4 %copy-start.22 = (f32[16,8,64]{2,1,0:T(8,128)S(1)}, f32[16,8,64]{2,1,0:T(8,128)}, u32[]{:S(2)}) copy-start(f32[16,8,64]{2,1,0:T(8,128)} %get-tuple-element.60) | copy-start | bytes 98308
  434.1 40.4 %copy-start.21 = (f32[16,8,64]{2,1,0:T(8,128)S(1)}, f32[16,8,64]{2,1,0:T(8,128)}, u32[]{:S(2)}) copy-start(f32[16,8,64]{2,1,0:T(8,128)} %get-tuple-element.59) | copy-start | bytes 98308
  434.1 40.5 %copy-start.7 = (f32[16,8,5,64]{3,1,0,2:T(8,128)S(1)}, f32[16,8,5,64]{3,1,0,2:T(8,128)}, u32[]{:S(2)}) copy-start(f32[16,8,5,64]{3,1,0,2:T(8,128)} %constant_dynamic-update-slice_fusion.10) | copy-start | bytes 491524
  434.1 40.5 %copy-start.23 = (f32[16,8,64]{2,1,0:T(8,128)S(1)}, f32[16,8,64]{2,1,0:T(8,128)}, u32[]{:S(2)}) copy-start(f32[16,8,64]{2,1,0:T(8,128)} %get-tuple-element.68) | copy-start | bytes 98308
  434.1 40.5 %copy-start.25 = (f32[16,8,64]{2,1,0:T(8,128)S(1)}, f32[16,8,64]{2,1,0:T(8,128)}, u32[]{:S(2)}) copy-start(f32[16,8,64]{2,1,0:T(8,128)} %get-tuple-element.70) | copy-start | bytes 98308
  434.1 40.5 %copy-start.26 = (f32[16,8,64]{2,1,0:T(8,128)S(1)}, f32[16,8,64]{2,1,0:T(8,128)}, u32[]{:S(2)}) copy-start(f32[16,8,64]{2,1,0:T(8,128)} %get-tuple-element.74) | copy-start | bytes 98308
  434.2 40.5 %copy-start.27 = (f32[16,8,64]{2,1,0:T(8,128)S(1)}, f32[16,8,64]{2,1,0:T(8,128)}, u32[]{:S(2)}) copy-start(f32[16,8,64]{2,1,0:T(8,128)} %get-tuple-element.72) | copy-start | bytes 98308
  445.8 28.9 %copy-start.11 = (f32[16,8,5,64]{3,1,0,2:T(8,128)S(1)}, f32[16,8,5,64]{3,1,0,2:T(8,128)}, u32[]{:S(2)}) copy-start(f32[16,8,5,64]{3,1,0,2:T(8,128)} %copy-done.10) | copy-start | bytes 491524
  445.8 28.9 %copy-start.28 = (f32[16,8,64]{2,1,0:T(8,128)S(1)}, f32[16,8,64]{2,1,0:T(8,128)}, u32[]{:S(2)}) copy-start(f32[16,8,64]{2,1,0:T(8,128)} %get-tuple-element.76) | copy-start | bytes 98308
  445.8 28.9 %copy-start.30 = (f32[16,8,64]{2,1,0:T(8,128)S(1)}, f32[16,8,64]{2,1,0:T(8,128)}, u32[]{:S(2)}) copy-start(f32[16,8,64]{2,1,0:T(8,128)} %get-tuple-element.85) | copy-start | bytes 98308
  445.8 28.9 %copy-start.9 = (f32[16,8,5,64]{3,1,0,2:T(8,128)S(1)}, f32[16,8,5,64]{3,1,0,2:T(8,128)}, u32[]{:S(2)}) copy-start(f32[16,8,5,64]{3,1,0,2:T(8,128)} %copy-done.8) | copy-start | bytes 491524
  445.8 28.9 %copy-start.24 = (f32[16,8,64]{2,1,0:T(8,128)S(1)}, f32[16,8,64]{2,1,0:T(8,128)}, u32[]{:S(2)}) copy-start(f32[16,8,64]{2,1,0:T(8,128)} %get-tuple-element.80) | copy-start | bytes 98308
  445.8 28.9 %copy-start.29 = (f32[16,8,64]{2,1,0:T(8,128)S(1)}, f32[16,8,64]{2,1,0:T(8,128)}, u32[]{:S(2)}) copy-start(f32[16,8,64]{2,1,0:T(8,128)} %get-tuple-element.78) | copy-start | bytes 98308
where the time goes:
time: 534 us; the launch traced here: 525 us
  other arithmetic  424 us (79%)
  local copies, waits for them, and re-layouts  66.5 us (12%)
  starting transfers between devices  31.6 us (6%)
    reduce_sum x9, other arithmetic, pair_sums(): jnp.sum(weighted * (viscous * diff_w - pressure * delta_z), axis=-1)  137 us
    reduce_sum x8, other arithmetic, pair_sums(): jnp.sum(weighted * (2.0 * KAPPA) * near[9] * far[9] * damping * (near[11]...  116 us
    reduce_sum x8, other arithmetic, pair_sums(): jnp.sum(weighted * (viscous * diff_u - pressure * delta_x), axis=-1)  93.8 us
    slice x8, other arithmetic, pair_sums(): far = [neighbour[..., k, None, :] for k in range(12)]  38.7 us
    reduce_sum x8, other arithmetic, wall_terms(): force_x = push * jnp.sum(corrected * wall_part[:, 3, None, :], axis=-1)  22.6 us
    reshape x8, local copies, waits for them, and re-layouts, neighbour_terms(): beside.reshape(rows_a, rows_b, 12, 64)  16 us
  transfers between devices with their start and end apart: 6, of which 0 were waited for; matrix products, arithmetic and copies ran while one was open for 83% of the time, Pallas kernels for 0%

commit v1 on v0

v1 whole, which is shorter than its diff:
```python
import math

import jax
import jax.numpy as jnp
from jax import lax
from jax.experimental import pallas as pl
from jax.experimental.pallas import tpu as pltpu
from jax.sharding import PartitionSpec as P

CA = 16
CB = 8
PAIRS = 4
SLOTS = 8
KERN_W = 21.0 / (16.0 * math.pi)
KERN_F = 105.0 / (16.0 * math.pi)
KAPPA = 0.02
WALL_PUSH = 0.03
WALL_HEAT = 0.02
EPS_R = 0.01
F32 = jnp.float32
BF16 = jnp.bfloat16


def iota(shape, axis):
    return lax.broadcasted_iota(jnp.int32, shape, axis)


def split2(value):
    high = value.astype(BF16)
    low = (value - high.astype(F32)).astype(BF16)
    return high, low


def split3(value):
    high = value.astype(BF16).astype(F32)
    rest = value - high
    middle = rest.astype(BF16).astype(F32)
    return high, middle, rest - middle


def pack_kernel(counts_ref, fluid_ref, out_ref):
    lane = iota((8, 128), 1)
    left = lane < 64
    slot = lane - jnp.where(left, 0, 64)

    def row(a, carry):
        comps = []
        for v in range(6):
            x = fluid_ref[a, :, v * 128 : (v + 1) * 128]
            turned = pltpu.roll(x, 64, 1)
            comps.append(jnp.where(left, x, pltpu.roll(turned, 7, 0)))
            comps.append(jnp.where(left, turned, pltpu.roll(x, 7, 0)))
        density, smooth, sound = comps[7], comps[8], comps[9]
        inverse = 1.0 / density
        d2 = density * density
        d4 = d2 * d2
        pressure = sound * sound / 7.0 * (d4 * d2 * density - 1.0)
        fields = comps[:6] + [
            comps[6],
            pressure * inverse * inverse,
            comps[10] * inverse,
            inverse,
            smooth,
            comps[11],
            sound,
        ]
        for p in range(PAIRS):
            count = jnp.where(left[:1], counts_ref[2 * p, a], counts_ref[2 * p + 1, a])
            for c, field in enumerate(fields):
                line = field[2 * p : 2 * p + 1]
                if c == 6:
                    line = jnp.where(slot[:1] < count, line, 0.0)
                out_ref[a, p, c : c + 1, :] = line
            out_ref[a, p, 13:16, :] = jnp.zeros((3, 128), F32)
        return carry

    lax.fori_loop(0, CA, row, 0)


def pack_records(fluid_state, counts_t):
    return pl.pallas_call(
        pack_kernel,
        out_shape=jax.ShapeDtypeStruct((CA, PAIRS, 16, 128), F32),
        in_specs=[
            pl.BlockSpec(memory_space=pltpu.SMEM),
            pl.BlockSpec(memory_space=pltpu.VMEM),
        ],
        out_specs=pl.BlockSpec(memory_space=pltpu.VMEM),
        name="pack_records",
    )(counts_t, fluid_state)


def route_kernel(devices, wall_ref, readers_ref, targets_ref, out_ref, sel_ref, rhs_ref):
    rows = wall_ref.shape[0]
    lane = iota((rows, 128), 1)
    left = lane < 64
    later = (iota((rows, rows), 0) < iota((rows, rows), 1)).astype(BF16)
    device = iota((devices, rows), 0)
    before = jnp.zeros((devices, 1), F32)
    slots = []
    cells = jnp.zeros((devices, 128), F32)
    slot_row = iota((128, rows), 0).astype(F32)
    for r in range(2):
        reader = readers_ref[r : r + 1, :]
        hot = (device == reader).astype(F32)
        earlier = jnp.dot(hot.astype(BF16), later, preferred_element_type=F32) + before
        position = jnp.sum(hot * earlier, axis=0, keepdims=True)
        before = before + jnp.sum(hot, axis=1, keepdims=True)
        slots.append(reader * SLOTS + position.astype(jnp.int32))
        named = jnp.where(slot_row == position, targets_ref[r : r + 1, :].astype(F32), 0.0)
        named = jnp.where(slot_row == SLOTS, 1.0, named)
        cells = cells + lax.dot_general(
            hot.astype(BF16),
            named.astype(BF16),
            (((1,), (1,)), ((), ())),
            preferred_element_type=F32,
        )
    chunk = devices * SLOTS // 2
    pair = iota((chunk, rows), 0) * 2
    for half in range(2):
        chosen = (pair + half == slots[0]) | (pair + half == slots[1])
        sel_ref[:, half * rows : (half + 1) * rows] = jnp.where(chosen, 1.0, 0.0).astype(BF16)
    gamma = wall_ref[:, 384:512]
    gamma = jnp.where(left, gamma, pltpu.roll(gamma, 64, 1))
    for v in range(4):
        x = wall_ref[:, v * 128 : (v + 1) * 128]
        if v == 1:
            x = jnp.where(left, x, x * gamma)
        elif v == 2:
            x = x * gamma
        elif v == 3:
            x = jnp.where(left, x, x * gamma)
        turned = pltpu.roll(x, 64, 1)
        for odd in range(2):
            even_half = jnp.where(left, turned if odd else x, 0.0)
            odd_half = jnp.where(left, 0.0, x if odd else turned)
            for part, (e, o) in enumerate(zip(split3(even_half), split3(odd_half))):
                rhs_ref[0:rows, part * 128 : (part + 1) * 128] = e.astype(BF16)
                rhs_ref[rows : 2 * rows, part * 128 : (part + 1) * 128] = o.astype(BF16)
            got = jnp.dot(sel_ref[...], rhs_ref[...], preferred_element_type=F32)
            got = got[:, 0:128] + got[:, 128:256] + got[:, 256:384]
            got = got.reshape(devices, SLOTS // 2, 128)
            for q in range(SLOTS // 2):
                out_ref[:, q * 8 + 2 * v + odd, :] = got[:, q, :]
    for k in range(8):
        out_ref[:, 32 + k, :] = cells


def route_walls(devices, wall_blocks, readers_t, targets_t):
    rows = wall_blocks.shape[0]
    return pl.pallas_call(
        lambda *refs: route_kernel(devices, *refs),
        out_shape=jax.ShapeDtypeStruct((devices, 40, 128), F32),
        in_specs=[pl.BlockSpec(memory_space=pltpu.VMEM)] * 3,
        out_specs=pl.BlockSpec(memory_space=pltpu.VMEM),
        scratch_shapes=[
            pltpu.VMEM((devices * SLOTS // 2, 2 * rows), BF16),
            pltpu.VMEM((2 * rows, 384), BF16),
        ],
        compiler_params=pltpu.CompilerParams(vmem_limit_bytes=40 << 20),
        name="route_walls",
    )(wall_blocks, readers_t, targets_t)


def features(tile, left):
    x = tile[0:1] - 0.5
    y = tile[1:2] + jnp.where(left, -1.0, 0.0)
    z = tile[2:3] - 2.0
    u, v, w = tile[3:4], tile[4:5], tile[5:6]
    mass = tile[6:7] * (-32.0 * KERN_F)
    mp = mass * tile[7:8]
    mv = mass * tile[8:9]
    mi = mass * tile[9:10]
    heat = tile[11:12]
    mu, mvv, mw = mass * u, mass * v, mass * w
    first = [mass, mp, mu, mass, mp, mvv, mw, mass * z]
    second = [mass * x, mp * x, mu * x, mass * y, mp * y, mvv * y, mp * z, mw * z]
    third = [mi, mi * u, mi * v, mi * w, mi * heat, mv, mv * u, mv * v]
    fourth = [mv * w] + [jnp.zeros_like(x)] * 7
    return (
        jnp.concatenate(first + second, axis=0),
        jnp.concatenate(third + fourth, axis=0),
        jnp.concatenate([x, y, z, tile[10:11]] + [jnp.zeros_like(x)] * 4, axis=0),
    )


def near_kernel(ext_ref, out_ref, feat_ref, turn_ref, am_ref, bm_ref, ax_ref, bx_ref):
    left1 = iota((1, 128), 1) < 64
    left16 = iota((16, 128), 1) < 64

    def prepare(k, carry):
        a = k // 6
        p = k - a * 6
        fa, fb, pos = features(ext_ref[a, p], left1)
        for variant in range(3):
            if variant == 0:
                va, vb = fa, fb
            else:
                ta, tb = pltpu.roll(fa, 64, 1), pltpu.roll(fb, 64, 1)
                keep = left16 if variant == 1 else jnp.logical_not(left16)
                va, vb = jnp.where(keep, fa, ta), jnp.where(keep, fb, tb)
            ha, la = split2(va)
            hb, lb = split2(vb)
            feat_ref[a, p, variant, 0:16, :] = ha
            feat_ref[a, p, variant, 16:32, :] = la
            feat_ref[a, p, variant, 32:48, :] = hb
            feat_ref[a, p, variant, 48:64, :] = lb
        turn_ref[a, p] = pos.T
        return carry

    lax.fori_loop(0, 18 * 6, prepare, 0)

    rows8 = iota((8, 128), 0)

    def kernel_rows(xi, yi, zi, hi, xj, yj, zj, hj):
        dx = xi - xj
        dy = yi - yj
        dz = zi - zj
        s = dx * dx + dy * dy + dz * dz
        wide = hi + hj
        w2 = wide * wide
        e = s + (0.25 * EPS_R) * w2
        w4 = w2 * w2
        den = w4 * w4 * e
        r = s * lax.rsqrt(jnp.maximum(s, 1e-30))
        shell = jnp.maximum(wide - r, 0.0)
        base = shell * shell * shell / den
        return split2(base * e), split2(base * s)

    def pair(k, carry):
        a = k // PAIRS
        p = k - a * PAIRS
        tile = ext_ref[a + 1, p + 1]
        x0 = tile[0:1] - 0.5
        yi = tile[1:2] + jnp.where(left1, -1.0, 0.0)
        zi = tile[2:3] - 2.0
        hi = tile[10:11]
        y_mixed = yi + jnp.where(left1, 2.0, -2.0)
        sums = [jnp.zeros((8, 128), F32) for _ in range(4)]
        for sx in (-1, 0, 1):
            r = a + 1 + sx
            xi = x0 - float(sx)
            for c in range(8):
                rows = pl.ds(c * 16, 16)
                t = turn_ref[r, p + 1, rows, :]
                (ah, al), (bh, bl) = kernel_rows(
                    xi, yi, zi, hi, t[:, 0:1], t[:, 1:2], t[:, 2:3], t[:, 3:4]
                )
                am_ref[sx + 1, c * 16 : c * 16 + 16, :] = ah
                am_ref[sx + 1, 128 + c * 16 : 144 + c * 16, :] = al
                bm_ref[sx + 1, c * 16 : c * 16 + 16, :] = bh
                bm_ref[sx + 1, 128 + c * 16 : 144 + c * 16, :] = bl
            for c in range(4):
                tl = turn_ref[r, p, pl.ds(64 + c * 16, 16), :]
                tr = turn_ref[r, p + 2, pl.ds(c * 16, 16), :]
                mixed = [jnp.where(left16, tl[:, n : n + 1], tr[:, n : n + 1]) for n in range(4)]
                (ah, al), (bh, bl) = kernel_rows(xi, y_mixed, zi, hi, *mixed)
                ax_ref[sx + 1, c * 16 : c * 16 + 16, :] = ah
                ax_ref[sx + 1, 64 + c * 16 : 80 + c * 16, :] = al
                bx_ref[sx + 1, c * 16 : c * 16 + 16, :] = bh
                bx_ref[sx + 1, 64 + c * 16 : 80 + c * 16, :] = bl
            mid = feat_ref[r, p + 1, 0]
            fa = jnp.concatenate([mid[0:32], mid[0:32]], axis=1)
            fb = jnp.concatenate([mid[32:64], mid[32:64]], axis=1)
            ga = jnp.dot(fa, am_ref[sx + 1], preferred_element_type=F32)
            gb = jnp.dot(fb, bm_ref[sx + 1], preferred_element_type=F32)
            side_l = feat_ref[r, p, 2]
            side_r = feat_ref[r, p + 2, 1]
            xa = jnp.dot(
                jnp.concatenate([side_l[0:32], side_r[0:32]], axis=0),
                ax_ref[sx + 1],
                preferred_element_type=F32,
            )
            xb = jnp.dot(
                jnp.concatenate([side_l[32:64], side_r[32:64]], axis=0),
                bx_ref[sx + 1],
                preferred_element_type=F32,
            )
            ga = ga[0:16] + ga[16:32]
            gb = gb[0:16] + gb[16:32]
            xa = jnp.where(left16, xa[0:16] + xa[16:32], xa[32:48] + xa[48:64])
            xb = jnp.where(left16, xb[0:16] + xb[16:32], xb[32:48] + xb[48:64])
            by_x = jnp.where(rows8 < 3, float(sx), 0.0)
            by_y = jnp.where((rows8 >= 3) & (rows8 < 6), jnp.where(left1, -2.0, 2.0), 0.0)
            sums[0] = sums[0] + (ga[0:8] + xa[0:8])
            sums[1] = sums[1] + (ga[8:16] + xa[8:16] + by_y * xa[0:8])
            if sx:
                sums[1] = sums[1] + by_x * (ga[0:8] + xa[0:8])
            sums[2] = sums[2] + (gb[0:8] + xb[0:8])
            sums[3] = sums[3] + (gb[8:16] + xb[8:16])
        v0, v1, v2, v3 = sums
        u, v, w = tile[3:4], tile[4:5], tile[5:6]
        sm, smp = v0[0:1], v0[1:2]
        gx = x0 * sm - v1[0:1]
        gy = yi * sm - v1[3:4]
        gz = zi * sm - v0[7:8]
        density = (
            u * gx
            - (x0 * v0[2:3] - v1[2:3])
            + v * gy
            - (yi * v0[5:6] - v1[5:6])
            + w * gz
            - (zi * v0[6:7] - v1[7:8])
        )
        pi, visc, inv = tile[7:8], tile[8:9], tile[9:10]
        smi, smv = v2[0:1], v2[5:6]
        ax = visc * (u * smi - v2[1:2]) + inv * (u * smv - v2[6:7])
        ay = visc * (v * smi - v2[2:3]) + inv * (v * smv - v2[7:8])
        az = visc * (w * smi - v2[3:4]) + inv * (w * smv - v3[0:1])
        ax = ax - (pi * gx + (x0 * smp - v1[1:2]))
        ay = ay - (pi * gy + (yi * smp - v1[4:5]))
        az = az - (pi * gz + (zi * smp - v1[6:7]))
        heat = (2.0 * KAPPA) * inv * (tile[11:12] * smi - v2[4:5])
        out_ref[a, p, 0:1, :] = density
        out_ref[a, p, 1:2, :] = ax
        out_ref[a, p, 2:3, :] = ay
        out_ref[a, p, 3:4, :] = az
        out_ref[a, p, 4:5, :] = heat
        out_ref[a, p, 5:8, :] = jnp.zeros((3, 128), F32)
        return carry

    lax.fori_loop(0, CA * PAIRS, pair, 0)


def near_terms(ext):
    return pl.pallas_call(
        near_kernel,
        out_shape=jax.ShapeDtypeStruct((CA, PAIRS, 8, 128), F32),
        in_specs=[pl.BlockSpec(memory_space=pltpu.VMEM)],
        out_specs=pl.BlockSpec(memory_space=pltpu.VMEM),
        scratch_shapes=[
            pltpu.VMEM((18, 6, 3, 64, 128), BF16),
            pltpu.VMEM((18, 6, 128, 8), F32),
            pltpu.VMEM((3, 256, 128), BF16),
            pltpu.VMEM((3, 256, 128), BF16),
            pltpu.VMEM((3, 128, 128), BF16),
            pltpu.VMEM((3, 128, 128), BF16),
        ],
        compiler_params=pltpu.CompilerParams(vmem_limit_bytes=48 << 20),
        name="near_terms",
    )(ext)


def wall_kernel(cells_ref, recv_ref, rec_ref, near_ref, rates_ref, dens_ref, lhs_ref, acc_ref):
    lane1 = iota((1, 128), 1)
    left1 = lane1 < 64
    row8 = iota((8, 128), 0)
    left8 = iota((8, 128), 1) < 64
    left16 = iota((16, 128), 1) < 64

    def cell_features(k, carry):
        a = k // PAIRS
        p = k - a * PAIRS
        tile = rec_ref[a, p]
        x = tile[0:1] - 0.5
        y = tile[1:2] - 0.5
        z = tile[2:3] - 2.0
        h = tile[10:11]
        s = 0.25 / (h * h)
        zero = jnp.zeros_like(x)
        rows = jnp.concatenate(
            [-2.0 * s * x, -2.0 * s * y, -2.0 * s * z, s, s * (x * x + y * y + z * z)] + [zero] * 3,
            axis=0,
        )
        hi, mid, lo = split3(rows)
        pad = jnp.zeros((16, 128), F32)
        stack = jnp.concatenate([hi, hi, mid, hi, mid, lo, pad], axis=0)
        both = jnp.concatenate([stack, stack], axis=0).T
        first = iota((128, 128), 1) < 64
        lhs_ref[2 * k, 0] = jnp.where(first[:64], both[:64], 0.0).astype(BF16)
        lhs_ref[2 * k, 1] = jnp.where(first[:64], 0.0, both[:64]).astype(BF16)
        lhs_ref[2 * k + 1, 0] = jnp.where(first[64:], both[64:], 0.0).astype(BF16)
        lhs_ref[2 * k + 1, 1] = jnp.where(first[64:], 0.0, both[64:]).astype(BF16)
        acc_ref[2 * k] = jnp.zeros((8, 128), F32)
        acc_ref[2 * k + 1] = jnp.zeros((8, 128), F32)
        return carry

    lax.fori_loop(0, CA * PAIRS, cell_features, 0)

    center = jnp.where(row8 == 2, 2.0, 0.5)

    def slot_pair(src, q):
        ca = cells_ref[src * 16 + 2 * q]
        cb = cells_ref[src * 16 + 2 * q + 1]
        tile = recv_ref[src, q * 8 : q * 8 + 8, :]
        c = tile - center
        sq = c * c
        norm = pltpu.roll(sq, 1, 0) + pltpu.roll(sq, 2, 0) + pltpu.roll(sq, 3, 0)
        rows = jnp.where(
            row8 < 3, c, jnp.where(row8 == 3, norm, jnp.where(row8 == 4, 1.0, 0.0))
        )
        hi, mid, lo = split3(rows)
        blocks = []
        for side in range(2):
            keep = left8 if side == 0 else jnp.logical_not(left8)
            h1, m1, l1 = [jnp.where(keep, t, 0.0) for t in (hi, mid, lo)]
            for top, bottom in ((h1, m1), (h1, l1), (m1, h1)):
                blocks.append(jnp.concatenate([top, bottom], axis=0).astype(BF16))
            blocks.append(jnp.zeros((16, 128), BF16))
        right = jnp.concatenate(blocks, axis=0)
        lhs = lhs_ref[ca, 0] + lhs_ref[cb, 1]
        q2 = jnp.maximum(jnp.dot(lhs, right, preferred_element_type=F32), 1e-30)
        t = q2 * lax.rsqrt(q2)
        shell = jnp.maximum(1.0 - t, 0.0)
        shell = shell * shell
        kernel = shell * shell * (4.0 * t + 1.0)
        kh, kl = split2(kernel)
        give = jnp.where(row8 < 3, 0.0, tile)
        gh, gl = split2(give)
        gh, gl = gh.astype(F32), gl.astype(F32)
        zero = jnp.zeros_like(gh)
        feats = jnp.concatenate(
            [
                jnp.concatenate([jnp.where(left8, gh, zero), jnp.where(left8, gl, zero)], axis=0),
                jnp.concatenate([jnp.where(left8, zero, gh), jnp.where(left8, zero, gl)], axis=0),
            ],
            axis=0,
        ).astype(BF16)
        got = lax.dot_general(
            feats,
            jnp.concatenate([kh, kl], axis=0),
            (((1,), (1,)), ((), ())),
            preferred_element_type=F32,
        )
        acc_ref[ca] = acc_ref[ca] + (got[0:8] + got[8:16])
        acc_ref[cb] = acc_ref[cb] + (got[16:24] + got[24:32])

    def source(src, carry):
        for q in range(SLOTS // 2):
            slot_pair(src, q)
        return carry

    lax.fori_loop(0, recv_ref.shape[0], source, 0)

    def finish(a, carry):
        for p in range(PAIRS):
            ta = acc_ref[a * CB + 2 * p]
            tb = acc_ref[a * CB + 2 * p + 1]
            total = jnp.where(left8, ta + pltpu.roll(ta, 64, 1), tb + pltpu.roll(tb, 64, 1))
            tile = rec_ref[a, p]
            near = near_ref[a, p]
            h, sound = tile[10:11], tile[12:13]
            scale = KERN_W / (h * h * h)
            push = WALL_PUSH * sound * sound * scale
            heat = WALL_HEAT * scale * (total[7:8] - tile[11:12] * total[6:7])
            r = [near[1 + n : 2 + n] + push * total[3 + n : 4 + n] for n in range(3)]
            r.append(near[4:5] + heat)
            t = [pltpu.roll(line, 64, 1) for line in r]
            for v in range(2):
                lo, hi = 2 * v, 2 * v + 1
                span = slice(v * 128, (v + 1) * 128)
                rates_ref[a, 2 * p : 2 * p + 1, span] = jnp.where(left1, r[lo], t[hi])
                rates_ref[a, 2 * p + 1 : 2 * p + 2, span] = jnp.where(left1, t[lo], r[hi])
            dens_ref[a, p : p + 1, :] = near[0:1]
        return carry

    lax.fori_loop(0, CA, finish, 0)


def wall_terms(cells, recv, records, near):
    return pl.pallas_call(
        wall_kernel,
        out_shape=(
            jax.ShapeDtypeStruct((CA, CB, 256), F32),
            jax.ShapeDtypeStruct((CA, PAIRS, 128), F32),
        ),
        in_specs=[pl.BlockSpec(memory_space=pltpu.SMEM)]
        + [pl.BlockSpec(memory_space=pltpu.VMEM)] * 3,
        out_specs=[pl.BlockSpec(memory_space=pltpu.VMEM)] * 2,
        scratch_shapes=[
            pltpu.VMEM((CA * CB, 2, 64, 128), BF16),
            pltpu.VMEM((CA * CB, 8, 128), F32),
        ],
        compiler_params=pltpu.CompilerParams(vmem_limit_bytes=48 << 20),
        name="wall_terms",
    )(cells, recv, records, near)


def shift_from(array, axis, step):
    peers = lax.axis_size(axis)
    up = [(i, i + 1) for i in range(peers - 1)]
    pairs = up if step > 0 else [(j, i) for i, j in up]
    return lax.ppermute(array, axis, pairs)


def local(fluid_state, cell_counts, wall_blocks, readers, targets):
    devices = lax.axis_size("gx") * lax.axis_size("gy")
    records = pack_records(fluid_state, cell_counts.T)
    send = route_walls(devices, wall_blocks, readers.T, targets.T)
    before = shift_from(records[:, PAIRS - 1 :], "gy", 1)
    after = shift_from(records[:, :1], "gy", -1)
    wide = jnp.concatenate([before, records, after], axis=1)
    above = shift_from(wide[CA - 1 :], "gx", 1)
    below = shift_from(wide[:1], "gx", -1)
    ext = jnp.concatenate([above, wide, below], axis=0)
    recv = lax.all_to_all(send, ("gx", "gy"), split_axis=0, concat_axis=0, tiled=True)
    cells = recv[:, 32, :16].astype(jnp.int32).reshape(-1)
    near = near_terms(ext)
    rates, density = wall_terms(cells, recv, records, near)
    return (rates, density.reshape(CA, CB * 64))


def solution(mesh):
    placed = (
        P("gx", "gy", None),
        P("gx", "gy"),
        P(("gx", "gy"), None),
        P(("gx", "gy"), None),
        P(("gx", "gy"), None),
    )
    return jax.shard_map(
        local,
        mesh=mesh,
        in_specs=placed,
        out_specs=(P("gx", "gy", None), P("gx", "gy")),
        check_vma=False,
    )
```

time: 534 us -> 217 us (0.41)
  the two profiles are of different devices: /device:TPU:99 before, /device:TPU:2 now
where the time goes in v1:
time: 217 us
  Pallas kernels  157 us (72%)
  waiting for transfers between devices  28 us (13%)
  starting transfers between devices  23.1 us (11%)
  local copies, waits for them, and re-layouts  5.66 us (3%)
    pallas_call x1, Pallas kernels, wall_terms(): pl.pallas_call(wall_kernel, out_shape=(jax.ShapeDtypeStruct((CA, CB, 256)...  78.1 us
    pallas_call x1, Pallas kernels, near_terms(): pl.pallas_call(near_kernel, out_shape=jax.ShapeDtypeStruct((CA, PAIRS, 8,...  72.3 us
    ppermute x4, waiting for transfers between devices, shift_from(): return lax.ppermute(array, axis, pairs)  28 us
    ppermute x4, starting transfers between devices, shift_from(): return lax.ppermute(array, axis, pairs)  12.6 us
    all_to_all x1, starting transfers between devices, local(): lax.all_to_all(send, ('gx', 'gy'), split_axis=0, concat_axis=0, tiled=True)  10.5 us
    unnamed x11, local copies, waits for them, and re-layouts  4.53 us
  transfers between devices with their start and end apart: 5, of which 2 were waited for; matrix products, arithmetic and copies ran while one was open for 1% of the time, Pallas kernels for 35%

profile of v1, /device:TPU:2, one launch (start us, length us, event | category | flops | bytes accessed | tf_op | source)
XLA Modules:
  0.0 216.9 jit_solution(5591785993855584852)
XLA Ops:
  0.6 0.0 copy-start.2
  0.6 1.0 copy-done.2
  1.7 0.0 copy-start.3
  1.7 0.7 copy-done.3
  2.4 0.0 copy-start.4
  2.4 0.7 copy-done.4
  3.0 3.9 %route_walls.1 = f32[128,40,128]{2,1,0:T(8,128)S(1)} custom-call(f32[256,512]{1,0:T(8,128)S(1)} %copy-done.2, s32[2,256]{1,0:T(2,128)S(1)} %bitcast.8, s32[2,256]{1,0:T(2,128)S(1)} %bitcast.9), custom_call_target="tpu_custom_call" | custom-call | tf_op jit(solution)/shard_map/route_walls/pallas_call | solution.py:151
  6.9 0.0 copy-start.1
  6.9 1.5 copy-done.1
  8.4 10.5 %all-to-all-start = ((f32[128,40,128]{2,1,0:T(8,128)}), f32[128,40,128]{2,1,0:T(8,128)S(1)}, u32[]{:S(2)}, u32[]{:S(2)}) async-start(f32[128,40,128]{2,1,0:T(8,128)} %copy-done.1), calls=%async_computation | async-start | bytes 5242880 | tf_op jit(solution)/shard_map/all_to_all | solution.py:496
  19.0 3.1 %pack_records.1.rec_ref = f32[16,4,16,128]{3,2,1,0:T(8,128)} custom-call(s32[8,16]{1,0:T(8,128)} %bitcast.11, f32[16,8,768]{2,1,0:T(8,128)} %fluid_ref.1), custom_call_target="tpu_custom_call" | custom-call | tf_op jit(solution)/shard_map/pack_records/pallas_call | solution.py:81
  22.0 0.0 copy-start
  22.0 1.0 fusion.1
  23.1 1.3 collective-permute-start.1
  24.4 4.6 %collective-permute-start = (f32[16,1,16,128]{3,2,1,0:T(8,128)S(1)}, f32[16,1,16,128]{3,2,1,0:T(8,128)S(1)}, u32[]{:S(2)}, u32[]{:S(2)}) collective-permute-start(f32[16,1,16,128]{3,2,1,0:T(8,128)S(1)} %get-tuple-element.8), channel_id=1, source_target_pairs={{0,1},{1,2},{2,3},{4,5},{5,6},{6,7},{8,9},{9,10},{10,11},{12,13},{... | collective-permute-start | bytes 393224 | tf_op jit(solution)/shard_map/ppermute | solution.py:483
  28.9 22.4 %collective-permute-done.1 = f32[16,1,16,128]{3,2,1,0:T(8,128)S(1)} collective-permute-done((f32[16,1,16,128]{3,2,1,0:T(8,128)S(1)}, f32[16,1,16,128]{3,2,1,0:T(8,128)S(1)}, u32[]{:S(2)}, u32[]{:S(2)}) %collective-permute-start.1) | collective-permute-done | bytes 131104 | tf_op jit(solution)/shard_map/ppermute | solution.py:483
  51.4 0.0 collective-permute-done
  51.4 0.8 pad_maximum_fusion.3
  52.2 4.8 %collective-permute-start.3 = (f32[1,6,16,128]{3,2,1,0:T(8,128)S(1)}, f32[1,6,16,128]{3,2,1,0:T(8,128)S(1)}, u32[]{:S(2)}, u32[]{:S(2)}) collective-permute-start(f32[1,6,16,128]{3,2,1,0:T(8,128)S(1)} %get-tuple-element.7), channel_id=1, source_target_pairs={{4,0},{8,4},{12,8},{16,12},{20,16},{24,20},{28,24},{32,28},{36,32}... | collective-permute-start | bytes 147464 | tf_op jit(solution)/shard_map/ppermute | solution.py:483
  57.0 1.9 collective-permute-start.2
  58.9 0.0 collective-permute-done.3
  58.9 5.6 %collective-permute-done.2 = f32[1,6,16,128]{3,2,1,0:T(8,128)S(1)} collective-permute-done((f32[1,6,16,128]{3,2,1,0:T(8,128)S(1)}, f32[1,6,16,128]{3,2,1,0:T(8,128)S(1)}, u32[]{:S(2)}, u32[]{:S(2)}) %collective-permute-start.2) | collective-permute-done | bytes 49184 | tf_op jit(solution)/shard_map/ppermute | solution.py:483
  64.5 1.1 pad_maximum_fusion.ext_ref
  65.7 72.3 %near_terms.1.near_ref = f32[16,4,8,128]{3,2,1,0:T(8,128)S(1)} custom-call(f32[18,6,16,128]{3,2,1,0:T(8,128)S(1)} %pad_maximum_fusion.ext_ref), custom_call_target="tpu_custom_call" | custom-call | tf_op jit(solution)/shard_map/near_terms/pallas_call | solution.py:326
  137.9 0.0 all-to-all-done.recv_ref
  137.9 0.2 fusion
  138.1 0.1 convert_element_type.8.cells_ref
  138.2 0.0 copy-done
  138.2 78.1 %wall_terms.1 = (f32[16,8,256]{2,1,0:T(8,128)}, f32[16,4,128]{2,1,0:T(4,128)S(1)}) custom-call(s32[2048]{0:T(1024)S(1)} %convert_element_type.8.cells_ref, f32[128,40,128]{2,1,0:T(8,128)S(1)} %all-to-all-done.recv_ref, f32[16,4,16,128]{3,2,1,0:T(8,128)S(1)} %copy-done, f32[16,4,8,128]{3,2,1,0:T(8,128)S(1)} %near_terms.1.near_ref), custom_call_target="tpu_custom_call" | custom-call | tf_op jit(solution)/shard_map/wall_terms/pallas_call | solution.py:461
  216.3 0.6 copy.9
Async XLA Ops:
  0.6 1.0 copy-start.2
  1.7 0.7 copy-start.3
  2.4 0.7 copy-start.4
  6.9 1.5 copy-start.1
  8.4 129.5 %all-to-all-start = ((f32[128,40,128]{2,1,0:T(8,128)}), f32[128,40,128]{2,1,0:T(8,128)S(1)}, u32[]{:S(2)}, u32[]{:S(2)}) async-start(f32[128,40,128]{2,1,0:T(8,128)} %copy-done.1), calls=%async_computation | async-start | bytes 5242880 | tf_op jit(solution)/shard_map/all_to_all | solution.py:496
  22.0 116.2 %copy-start = (f32[16,4,16,128]{3,2,1,0:T(8,128)S(1)}, f32[16,4,16,128]{3,2,1,0:T(8,128)}, u32[]{:S(2)}) copy-start(f32[16,4,16,128]{3,2,1,0:T(8,128)} %pack_records.1.rec_ref) | copy-start | bytes 1572868
  23.1 28.3 %collective-permute-start.1 = (f32[16,1,16,128]{3,2,1,0:T(8,128)S(1)}, f32[16,1,16,128]{3,2,1,0:T(8,128)S(1)}, u32[]{:S(2)}, u32[]{:S(2)}) collective-permute-start(f32[16,1,16,128]{3,2,1,0:T(8,128)S(1)} %get-tuple-element.9), channel_id=1, source_target_pairs={{1,0},{2,1},{3,2},{5,4},{6,5},{7,6},{9,8},{10,9},{11,10},{13,12},{... | collective-permute-start | bytes 393224 | tf_op jit(solution)/shard_map/ppermute | solution.py:483
  24.4 27.0 %collective-permute-start = (f32[16,1,16,128]{3,2,1,0:T(8,128)S(1)}, f32[16,1,16,128]{3,2,1,0:T(8,128)S(1)}, u32[]{:S(2)}, u32[]{:S(2)}) collective-permute-start(f32[16,1,16,128]{3,2,1,0:T(8,128)S(1)} %get-tuple-element.8), channel_id=1, source_target_pairs={{0,1},{1,2},{2,3},{4,5},{5,6},{6,7},{8,9},{9,10},{10,11},{12,13},{... | collective-permute-start | bytes 393224 | tf_op jit(solution)/shard_map/ppermute | solution.py:483
  52.2 6.8 %collective-permute-start.3 = (f32[1,6,16,128]{3,2,1,0:T(8,128)S(1)}, f32[1,6,16,128]{3,2,1,0:T(8,128)S(1)}, u32[]{:S(2)}, u32[]{:S(2)}) collective-permute-start(f32[1,6,16,128]{3,2,1,0:T(8,128)S(1)} %get-tuple-element.7), channel_id=1, source_target_pairs={{4,0},{8,4},{12,8},{16,12},{20,16},{24,20},{28,24},{32,28},{36,32}... | collective-permute-start | bytes 147464 | tf_op jit(solution)/shard_map/ppermute | solution.py:483
  57.0 7.5 %collective-permute-start.2 = (f32[1,6,16,128]{3,2,1,0:T(8,128)S(1)}, f32[1,6,16,128]{3,2,1,0:T(8,128)S(1)}, u32[]{:S(2)}, u32[]{:S(2)}) collective-permute-start(f32[1,6,16,128]{3,2,1,0:T(8,128)S(1)} %get-tuple-element.6), channel_id=1, source_target_pairs={{0,4},{4,8},{8,12},{12,16},{16,20},{20,24},{24,28},{28,32},{32,36}... | collective-permute-start | bytes 147464 | tf_op jit(solution)/shard_map/ppermute | solution.py:483

commit v2 on v1

--- a/solution.py
+++ b/solution.py
@@ -162,126 +162,194 @@
     )(wall_blocks, readers_t, targets_t)
 
 
-def features(tile, left):
-    x = tile[0:1] - 0.5
-    y = tile[1:2] + jnp.where(left, -1.0, 0.0)
-    z = tile[2:3] - 2.0
-    u, v, w = tile[3:4], tile[4:5], tile[5:6]
-    mass = tile[6:7] * (-32.0 * KERN_F)
-    mp = mass * tile[7:8]
-    mv = mass * tile[8:9]
-    mi = mass * tile[9:10]
-    heat = tile[11:12]
-    mu, mvv, mw = mass * u, mass * v, mass * w
-    first = [mass, mp, mu, mass, mp, mvv, mw, mass * z]
-    second = [mass * x, mp * x, mu * x, mass * y, mp * y, mvv * y, mp * z, mw * z]
-    third = [mi, mi * u, mi * v, mi * w, mi * heat, mv, mv * u, mv * v]
-    fourth = [mv * w] + [jnp.zeros_like(x)] * 7
-    return (
-        jnp.concatenate(first + second, axis=0),
-        jnp.concatenate(third + fourth, axis=0),
-        jnp.concatenate([x, y, z, tile[10:11]] + [jnp.zeros_like(x)] * 4, axis=0),
-    )
-
-
-def near_kernel(ext_ref, out_ref, feat_ref, turn_ref, am_ref, bm_ref, ax_ref, bx_ref):
+def stack_rows(row8, rows):
+    out = jnp.broadcast_to(rows[0], row8.shape)
+    for n in range(1, len(rows)):
+        out = jnp.where(row8 == n, rows[n], out)
+    return out
+
+
+def groups(high, middle, low, order):
+    parts = {"h": high, "m": middle, "l": low}
+    return [
+        jnp.concatenate([parts[pair[0]], parts[pair[1]]], axis=0).astype(BF16) for pair in order
+    ]
+
+
+LEFT_ORDER = ("hh", "mh", "ml")
+RIGHT_ORDER = ("hm", "hl", "mh")
+
+
+def near_kernel(
+    ext_ref, out_ref, feat_ref, turn_ref, side_ref, geo_ref, sd0, mid0, mix0, sd1, mid1, mix1
+):
     left1 = iota((1, 128), 1) < 64
+    left8 = iota((8, 128), 1) < 64
     left16 = iota((16, 128), 1) < 64
-
-    def prepare(k, carry):
-        a = k // 6
-        p = k - a * 6
-        fa, fb, pos = features(ext_ref[a, p], left1)
-        for variant in range(3):
+    row8 = iota((8, 128), 0)
+    zero8 = jnp.zeros((8, 128), F32)
+    zero16 = jnp.zeros((16, 128), BF16)
+    own = jnp.where(left1, -1.0, 0.0)
+
+    def prepare(a, p):
+        row = lambda c: ext_ref[a, p, c : c + 1, :]
+        x = row(0) - 0.5
+        y = row(1) + own
+        z = row(2) - 2.0
+        u, v, w, mass = row(3), row(4), row(5), row(6) * (-32.0 * KERN_F)
+        pres, visc, inv, h, heat = row(7), row(8), row(9), row(10), row(11)
+        one = jnp.ones_like(x)
+        head = [one, pres, u, one, pres, v]
+        v0 = mass * stack_rows(row8, head + [w, z])
+        place = jnp.where(row8 < 3, x, jnp.where(row8 < 6, y, z))
+        v1 = mass * stack_rows(row8, head + [pres, w]) * place
+        v2 = mass * jnp.where(row8 < 5, inv, visc)
+        v2 = v2 * stack_rows(row8, [one, u, v, w, heat, one, u, v])
+        v3 = jnp.where(row8 == 0, mass * visc * w, 0.0)
+        fa = jnp.concatenate([v0, v1], axis=0)
+        fb = jnp.concatenate([v2, v3], axis=0)
+        turned = [pltpu.roll(t, 64, 1) for t in (v0, v1, v2, v3)]
+        ta = jnp.concatenate(turned[:2], axis=0)
+        tb = jnp.concatenate(turned[2:], axis=0)
+        for variant in ((2,) if p == 0 else (1,) if p == 5 else (0, 1, 2)):
             if variant == 0:
                 va, vb = fa, fb
+            elif variant == 1:
+                va, vb = jnp.where(left16, fa, ta), jnp.where(left16, fb, tb)
             else:
-                ta, tb = pltpu.roll(fa, 64, 1), pltpu.roll(fb, 64, 1)
-                keep = left16 if variant == 1 else jnp.logical_not(left16)
-                va, vb = jnp.where(keep, fa, ta), jnp.where(keep, fb, tb)
+                va, vb = jnp.where(left16, ta, fa), jnp.where(left16, tb, fb)
             ha, la = split2(va)
             hb, lb = split2(vb)
             feat_ref[a, p, variant, 0:16, :] = ha
             feat_ref[a, p, variant, 16:32, :] = la
             feat_ref[a, p, variant, 32:48, :] = hb
             feat_ref[a, p, variant, 48:64, :] = lb
-        turn_ref[a, p] = pos.T
+        norm = x * x + y * y + z * z
+        tile = stack_rows(row8, [x, y, z, one, norm, h, one, jnp.zeros_like(x)])
+        geo_ref[a, p] = stack_rows(row8, [x, y, z, norm, h, jnp.zeros_like(x)])
+        half = jnp.concatenate(groups(*split3(tile), LEFT_ORDER) + [zero16], axis=0)
+        turn_ref[a, p] = jnp.concatenate([half, half], axis=0).T
+
+    def prepare_row(a, carry):
+        for p in range(6):
+            prepare(a, p)
         return carry
 
-    lax.fori_loop(0, 18 * 6, prepare, 0)
-
-    rows8 = iota((8, 128), 0)
-
-    def kernel_rows(xi, yi, zi, hi, xj, yj, zj, hj):
-        dx = xi - xj
-        dy = yi - yj
-        dz = zi - zj
-        s = dx * dx + dy * dy + dz * dz
-        wide = hi + hj
+    lax.fori_loop(0, 18, prepare_row, 0)
+
+    def sides(a, carry):
+        for p in range(PAIRS):
+            keep = iota((64, 128), 1) < 64
+            side_ref[a, p] = jnp.where(
+                keep,
+                turn_ref[a, p, 64:128, :].astype(F32),
+                turn_ref[a, p + 2, 0:64, :].astype(F32),
+            ).astype(BF16)
+        return carry
+
+    lax.fori_loop(0, 18, sides, 0)
+
+    row16 = iota((16, 128), 0)
+    lane16 = iota((16, 128), 1)
+
+    def scalars(s, wide, diagonal):
+        s = jnp.maximum(s, 1e-20)
         w2 = wide * wide
         e = s + (0.25 * EPS_R) * w2
         w4 = w2 * w2
         den = w4 * w4 * e
-        r = s * lax.rsqrt(jnp.maximum(s, 1e-30))
-        shell = jnp.maximum(wide - r, 0.0)
+        shell = jnp.maximum(wide - s * lax.rsqrt(s), 0.0)
         base = shell * shell * shell / den
-        return split2(base * e), split2(base * s)
-
-    def pair(k, carry):
+        plain = base * e
+        if diagonal is not None:
+            plain = jnp.where(diagonal, 0.0, plain)
+        return split2(plain), split2(base * s)
+
+    y_shift = jnp.where(left1, -2.0, 2.0)
+    geo_mask = jnp.where(row8 < 3, -2.0, 0.0)
+    halves = lambda parts: (
+        groups(*[jnp.where(left8, t, 0.0) for t in parts], RIGHT_ORDER)
+        + [zero16]
+        + groups(*[jnp.where(left8, 0.0, t) for t in parts], RIGHT_ORDER)
+        + [zero16]
+    )
+
+    def distances(k, sd_ref):
         a = k // PAIRS
         p = k - a * PAIRS
-        tile = ext_ref[a + 1, p + 1]
-        x0 = tile[0:1] - 0.5
-        yi = tile[1:2] + jnp.where(left1, -1.0, 0.0)
-        zi = tile[2:3] - 2.0
-        hi = tile[10:11]
-        y_mixed = yi + jnp.where(left1, 2.0, -2.0)
-        sums = [jnp.zeros((8, 128), F32) for _ in range(4)]
+        geo = lambda c: geo_ref[a + 1, p + 1, c : c + 1, :]
+        x, y, norm, h = geo(0), geo(1), geo(3), geo(4)
+        flat = geo_ref[a + 1, p + 1] * geo_mask
+        wide_parts = split3(jnp.where(row8 == 5, 1.0, jnp.where(row8 == 6, h, 0.0)))
+        wide_mid = jnp.concatenate(groups(*wide_parts, RIGHT_ORDER) + [zero16], axis=0)
+        wide_mix = jnp.concatenate(halves(wide_parts), axis=0)
         for sx in (-1, 0, 1):
             r = a + 1 + sx
-            xi = x0 - float(sx)
-            for c in range(8):
-                rows = pl.ds(c * 16, 16)
-                t = turn_ref[r, p + 1, rows, :]
-                (ah, al), (bh, bl) = kernel_rows(
-                    xi, yi, zi, hi, t[:, 0:1], t[:, 1:2], t[:, 2:3], t[:, 3:4]
+            at = (sx + 1) * 192
+            n = norm - (2.0 * sx) * x + float(sx * sx) if sx else norm
+            base = flat + jnp.where(row8 == 0, 2.0 * sx, jnp.where(row8 == 4, 1.0, 0.0))
+            tile = jnp.where(row8 == 3, n, base)
+            right = jnp.concatenate(groups(*split3(tile), RIGHT_ORDER) + [zero16], axis=0)
+            sd_ref[at : at + 128, :] = jnp.dot(
+                turn_ref[r, p + 1][:, 0:64],
+                jnp.concatenate([right, wide_mid], axis=1),
+                preferred_element_type=F32,
+            )
+            nm = n - 2.0 * y_shift * y + 4.0
+            tile = jnp.where(row8 == 3, nm, base + jnp.where(row8 == 1, 2.0 * y_shift, 0.0))
+            right = jnp.concatenate(halves(split3(tile)), axis=0)
+            sd_ref[at + 128 : at + 192, :] = jnp.dot(
+                side_ref[r, p],
+                jnp.concatenate([right, wide_mix], axis=1),
+                preferred_element_type=F32,
+            )
+
+    def weigh(sd_ref, mid_ref, mix_ref):
+        for t in range(3):
+            for c in range(12):
+                at = t * 192 + c * 16
+                diagonal = (row16 + c * 16 == lane16) if t == 1 and c < 8 else None
+                (ah, al), (bh, bl) = scalars(
+                    sd_ref[at : at + 16, 0:128], sd_ref[at : at + 16, 128:256], diagonal
                 )
-                am_ref[sx + 1, c * 16 : c * 16 + 16, :] = ah
-                am_ref[sx + 1, 128 + c * 16 : 144 + c * 16, :] = al
-                bm_ref[sx + 1, c * 16 : c * 16 + 16, :] = bh
-                bm_ref[sx + 1, 128 + c * 16 : 144 + c * 16, :] = bl
-            for c in range(4):
-                tl = turn_ref[r, p, pl.ds(64 + c * 16, 16), :]
-                tr = turn_ref[r, p + 2, pl.ds(c * 16, 16), :]
-                mixed = [jnp.where(left16, tl[:, n : n + 1], tr[:, n : n + 1]) for n in range(4)]
-                (ah, al), (bh, bl) = kernel_rows(xi, y_mixed, zi, hi, *mixed)
-                ax_ref[sx + 1, c * 16 : c * 16 + 16, :] = ah
-                ax_ref[sx + 1, 64 + c * 16 : 80 + c * 16, :] = al
-                bx_ref[sx + 1, c * 16 : c * 16 + 16, :] = bh
-                bx_ref[sx + 1, 64 + c * 16 : 80 + c * 16, :] = bl
+                if c < 8:
+                    lo, step, ref = c * 16, 128, mid_ref
+                else:
+                    lo, step, ref = (c - 8) * 16, 64, mix_ref
+                ref[t, 0, lo : lo + 16, :] = ah
+                ref[t, 0, step + lo : step + lo + 16, :] = al
+                ref[t, 1, lo : lo + 16, :] = bh
+                ref[t, 1, step + lo : step + lo + 16, :] = bl
+
+    def gather(k, mid_ref, mix_ref):
+        a = k // PAIRS
+        p = k - a * PAIRS
+        sums = [zero8 for _ in range(4)]
+        for sx in (-1, 0, 1):
+            r = a + 1 + sx
             mid = feat_ref[r, p + 1, 0]
             fa = jnp.concatenate([mid[0:32], mid[0:32]], axis=1)
             fb = jnp.concatenate([mid[32:64], mid[32:64]], axis=1)
-            ga = jnp.dot(fa, am_ref[sx + 1], preferred_element_type=F32)
-            gb = jnp.dot(fb, bm_ref[sx + 1], preferred_element_type=F32)
+            ga = jnp.dot(fa, mid_ref[sx + 1, 0], preferred_element_type=F32)
+            gb = jnp.dot(fb, mid_ref[sx + 1, 1], preferred_element_type=F32)
             side_l = feat_ref[r, p, 2]
             side_r = feat_ref[r, p + 2, 1]
             xa = jnp.dot(
                 jnp.concatenate([side_l[0:32], side_r[0:32]], axis=0),
-                ax_ref[sx + 1],
+                mix_ref[sx + 1, 0],
                 preferred_element_type=F32,
             )
             xb = jnp.dot(
                 jnp.concatenate([side_l[32:64], side_r[32:64]], axis=0),
-                bx_ref[sx + 1],
+                mix_ref[sx + 1, 1],
                 preferred_element_type=F32,
             )
             ga = ga[0:16] + ga[16:32]
             gb = gb[0:16] + gb[16:32]
             xa = jnp.where(left16, xa[0:16] + xa[16:32], xa[32:48] + xa[48:64])
             xb = jnp.where(left16, xb[0:16] + xb[16:32], xb[32:48] + xb[48:64])
-            by_x = jnp.where(rows8 < 3, float(sx), 0.0)
-            by_y = jnp.where((rows8 >= 3) & (rows8 < 6), jnp.where(left1, -2.0, 2.0), 0.0)
+            by_x = jnp.where(row8 < 3, float(sx), 0.0)
+            by_y = jnp.where((row8 >= 3) & (row8 < 6), y_shift, 0.0)
             sums[0] = sums[0] + (ga[0:8] + xa[0:8])
             sums[1] = sums[1] + (ga[8:16] + xa[8:16] + by_y * xa[0:8])
             if sx:
@@ -289,37 +357,52 @@
             sums[2] = sums[2] + (gb[0:8] + xb[0:8])
             sums[3] = sums[3] + (gb[8:16] + xb[8:16])
         v0, v1, v2, v3 = sums
-        u, v, w = tile[3:4], tile[4:5], tile[5:6]
+        geo = lambda c: geo_ref[a + 1, p + 1, c : c + 1, :]
+        x, y, z = geo(0), geo(1), geo(2)
+        row = lambda c: ext_ref[a + 1, p + 1, c : c + 1, :]
+        u, v, w = row(3), row(4), row(5)
         sm, smp = v0[0:1], v0[1:2]
-        gx = x0 * sm - v1[0:1]
-        gy = yi * sm - v1[3:4]
-        gz = zi * sm - v0[7:8]
+        gx = x * sm - v1[0:1]
+        gy = y * sm - v1[3:4]
+        gz = z * sm - v0[7:8]
         density = (
             u * gx
-            - (x0 * v0[2:3] - v1[2:3])
+            - (x * v0[2:3] - v1[2:3])
             + v * gy
-            - (yi * v0[5:6] - v1[5:6])
+            - (y * v0[5:6] - v1[5:6])
             + w * gz
-            - (zi * v0[6:7] - v1[7:8])
+            - (z * v0[6:7] - v1[7:8])
         )
-        pi, visc, inv = tile[7:8], tile[8:9], tile[9:10]
+        pi, visc, inv = row(7), row(8), row(9)
         smi, smv = v2[0:1], v2[5:6]
         ax = visc * (u * smi - v2[1:2]) + inv * (u * smv - v2[6:7])
         ay = visc * (v * smi - v2[2:3]) + inv * (v * smv - v2[7:8])
         az = visc * (w * smi - v2[3:4]) + inv * (w * smv - v3[0:1])
-        ax = ax - (pi * gx + (x0 * smp - v1[1:2]))
-        ay = ay - (pi * gy + (yi * smp - v1[4:5]))
-        az = az - (pi * gz + (zi * smp - v1[6:7]))
-        heat = (2.0 * KAPPA) * inv * (tile[11:12] * smi - v2[4:5])
-        out_ref[a, p, 0:1, :] = density
-        out_ref[a, p, 1:2, :] = ax
-        out_ref[a, p, 2:3, :] = ay
-        out_ref[a, p, 3:4, :] = az
-        out_ref[a, p, 4:5, :] = heat
-        out_ref[a, p, 5:8, :] = jnp.zeros((3, 128), F32)
+        ax = ax - (pi * gx + (x * smp - v1[1:2]))
+        ay = ay - (pi * gy + (y * smp - v1[4:5]))
+        az = az - (pi * gz + (z * smp - v1[6:7]))
+        heat = (2.0 * KAPPA) * inv * (row(11) * smi - v2[4:5])
+        for n, line in enumerate((density, ax, ay, az, heat)):
+            out_ref[a, p, n : n + 1, :] = line
+
+    last = CA * PAIRS - 1
+    slots = ((sd0, mid0, mix0), (sd1, mid1, mix1))
+    for _, mid_ref, mix_ref in slots:
+        mid_ref[...] = jnp.zeros(mid_ref.shape, BF16)
+        mix_ref[...] = jnp.zeros(mix_ref.shape, BF16)
+    distances(0, sd0)
+
+    def step(m, carry):
+        for odd in range(2):
+            k = 2 * m + odd
+            sd_ref, mid_ref, mix_ref = slots[odd]
+            sd_next, mid_last, mix_last = slots[1 - odd]
+            gather(jnp.clip(k - 1, 0, last), mid_last, mix_last)
+            distances(jnp.minimum(k + 1, last), sd_next)
+            weigh(sd_ref, mid_ref, mix_ref)
         return carry
 
-    lax.fori_loop(0, CA * PAIRS, pair, 0)
+    lax.fori_loop(0, CA * PAIRS // 2 + 1, step, 0)
 
 
 def near_terms(ext):
@@ -330,107 +413,122 @@
         out_specs=pl.BlockSpec(memory_space=pltpu.VMEM),
         scratch_shapes=[
             pltpu.VMEM((18, 6, 3, 64, 128), BF16),
-            pltpu.VMEM((18, 6, 128, 8), F32),
-            pltpu.VMEM((3, 256, 128), BF16),
-            pltpu.VMEM((3, 256, 128), BF16),
-            pltpu.VMEM((3, 128, 128), BF16),
-            pltpu.VMEM((3, 128, 128), BF16),
-        ],
+            pltpu.VMEM((18, 6, 128, 128), BF16),
+            pltpu.VMEM((18, PAIRS, 64, 128), BF16),
+            pltpu.VMEM((18, 6, 8, 128), F32),
+        ]
+        + [
+            pltpu.VMEM((576, 256), F32),
+            pltpu.VMEM((3, 2, 256, 128), BF16),
+            pltpu.VMEM((3, 2, 128, 128), BF16),
+        ]
+        * 2,
         compiler_params=pltpu.CompilerParams(vmem_limit_bytes=48 << 20),
         name="near_terms",
     )(ext)
 
 
-def wall_kernel(cells_ref, recv_ref, rec_ref, near_ref, rates_ref, dens_ref, lhs_ref, acc_ref):
+UNROLL = 16
+
+
+def wall_kernel(cells_ref, recv_ref, rec_ref, near_ref, rates_ref, dens_ref, lhs_ref, acc_ref, list_ref):
     lane1 = iota((1, 128), 1)
     left1 = lane1 < 64
     row8 = iota((8, 128), 0)
     left8 = iota((8, 128), 1) < 64
-    left16 = iota((16, 128), 1) < 64
+    zero8 = jnp.zeros((8, 128), F32)
+    zero16 = jnp.zeros((16, 128), BF16)
+
+    def listing(src, m):
+        for q in range(SLOTS // 2):
+            list_ref[m + q] = src * (SLOTS // 2) + q
+        return m + (cells_ref[src * 16 + SLOTS] + 1) // 2
+
+    live = lax.fori_loop(0, recv_ref.shape[0], listing, 0)
+    for q in range(UNROLL):
+        list_ref[live + q] = 0
 
     def cell_features(k, carry):
         a = k // PAIRS
         p = k - a * PAIRS
-        tile = rec_ref[a, p]
-        x = tile[0:1] - 0.5
-        y = tile[1:2] - 0.5
-        z = tile[2:3] - 2.0
-        h = tile[10:11]
+        row = lambda c: rec_ref[a, p, c : c + 1, :]
+        x = row(0) - 0.5
+        y = row(1) - 0.5
+        z = row(2) - 2.0
+        h = row(10)
         s = 0.25 / (h * h)
-        zero = jnp.zeros_like(x)
-        rows = jnp.concatenate(
-            [-2.0 * s * x, -2.0 * s * y, -2.0 * s * z, s, s * (x * x + y * y + z * z)] + [zero] * 3,
-            axis=0,
+        norm = x * x + y * y + z * z
+        rows = s * stack_rows(
+            row8, [-2.0 * x, -2.0 * y, -2.0 * z, jnp.ones_like(x), norm, jnp.zeros_like(x)]
         )
-        hi, mid, lo = split3(rows)
-        pad = jnp.zeros((16, 128), F32)
-        stack = jnp.concatenate([hi, hi, mid, hi, mid, lo, pad], axis=0)
-        both = jnp.concatenate([stack, stack], axis=0).T
-        first = iota((128, 128), 1) < 64
-        lhs_ref[2 * k, 0] = jnp.where(first[:64], both[:64], 0.0).astype(BF16)
-        lhs_ref[2 * k, 1] = jnp.where(first[:64], 0.0, both[:64]).astype(BF16)
-        lhs_ref[2 * k + 1, 0] = jnp.where(first[64:], both[64:], 0.0).astype(BF16)
-        lhs_ref[2 * k + 1, 1] = jnp.where(first[64:], 0.0, both[64:]).astype(BF16)
-        acc_ref[2 * k] = jnp.zeros((8, 128), F32)
-        acc_ref[2 * k + 1] = jnp.zeros((8, 128), F32)
+        half = jnp.concatenate(groups(*split3(rows), LEFT_ORDER) + [zero16], axis=0)
+        both = jnp.concatenate([half, half], axis=0).T
+        lhs_ref[2 * k] = both[:64]
+        lhs_ref[2 * k + 1] = both[64:]
+        acc_ref[2 * k] = zero8
+        acc_ref[2 * k + 1] = zero8
         return carry
 
     lax.fori_loop(0, CA * PAIRS, cell_features, 0)
 
-    center = jnp.where(row8 == 2, 2.0, 0.5)
-
-    def slot_pair(src, q):
-        ca = cells_ref[src * 16 + 2 * q]
-        cb = cells_ref[src * 16 + 2 * q + 1]
-        tile = recv_ref[src, q * 8 : q * 8 + 8, :]
-        c = tile - center
-        sq = c * c
-        norm = pltpu.roll(sq, 1, 0) + pltpu.roll(sq, 2, 0) + pltpu.roll(sq, 3, 0)
-        rows = jnp.where(
-            row8 < 3, c, jnp.where(row8 == 3, norm, jnp.where(row8 == 4, 1.0, 0.0))
-        )
-        hi, mid, lo = split3(rows)
-        blocks = []
-        for side in range(2):
-            keep = left8 if side == 0 else jnp.logical_not(left8)
-            h1, m1, l1 = [jnp.where(keep, t, 0.0) for t in (hi, mid, lo)]
-            for top, bottom in ((h1, m1), (h1, l1), (m1, h1)):
-                blocks.append(jnp.concatenate([top, bottom], axis=0).astype(BF16))
-            blocks.append(jnp.zeros((16, 128), BF16))
-        right = jnp.concatenate(blocks, axis=0)
-        lhs = lhs_ref[ca, 0] + lhs_ref[cb, 1]
-        q2 = jnp.maximum(jnp.dot(lhs, right, preferred_element_type=F32), 1e-30)
-        t = q2 * lax.rsqrt(q2)
-        shell = jnp.maximum(1.0 - t, 0.0)
-        shell = shell * shell
-        kernel = shell * shell * (4.0 * t + 1.0)
-        kh, kl = split2(kernel)
-        give = jnp.where(row8 < 3, 0.0, tile)
-        gh, gl = split2(give)
-        gh, gl = gh.astype(F32), gl.astype(F32)
-        zero = jnp.zeros_like(gh)
-        feats = jnp.concatenate(
-            [
-                jnp.concatenate([jnp.where(left8, gh, zero), jnp.where(left8, gl, zero)], axis=0),
-                jnp.concatenate([jnp.where(left8, zero, gh), jnp.where(left8, zero, gl)], axis=0),
-            ],
-            axis=0,
-        ).astype(BF16)
-        got = lax.dot_general(
-            feats,
-            jnp.concatenate([kh, kl], axis=0),
-            (((1,), (1,)), ((), ())),
-            preferred_element_type=F32,
-        )
-        acc_ref[ca] = acc_ref[ca] + (got[0:8] + got[8:16])
-        acc_ref[cb] = acc_ref[cb] + (got[16:24] + got[24:32])
-
-    def source(src, carry):
-        for q in range(SLOTS // 2):
-            slot_pair(src, q)
+    center = jnp.where(row8 == 2, 2.0, jnp.where(row8 < 2, 0.5, 0.0))
+
+    def block(k, carry):
+        ids, tiles, squares = [], [], []
+        for u in range(UNROLL):
+            at = k * UNROLL + u
+            pair = list_ref[at]
+            src = pair // (SLOTS // 2)
+            q = pair - src * (SLOTS // 2)
+            ca = cells_ref[src * 16 + 2 * q]
+            cb = cells_ref[src * 16 + 2 * q + 1]
+            ids.append((ca, cb))
+            tile = recv_ref[src, pl.ds(pl.multiple_of(q * 8, 8), 8), :]
+            tiles.append(jnp.where(at < live, tile, 0.0))
+            c = tile - center
+            sq = c * c
+            norm = sq[0:1] + sq[1:2] + sq[2:3]
+            rows = jnp.where(
+                row8 < 3, c, jnp.where(row8 == 3, norm, jnp.where(row8 == 4, 1.0, 0.0))
+            )
+            parts = split3(rows)
+            lefts = groups(*[jnp.where(left8, t, 0.0) for t in parts], RIGHT_ORDER) + [zero16]
+            rights = groups(*[jnp.where(left8, 0.0, t) for t in parts], RIGHT_ORDER) + [zero16]
+            right = jnp.concatenate(lefts + rights, axis=0)
+            lhs = jnp.concatenate([lhs_ref[ca][:, 0:64], lhs_ref[cb][:, 64:128]], axis=1)
+            squares.append(jnp.dot(lhs, right, preferred_element_type=F32))
+        weights = []
+        for u in range(UNROLL):
+            q2 = jnp.maximum(squares[u], 1e-20)
+            t = q2 * lax.rsqrt(q2)
+            shell = jnp.maximum(1.0 - t, 0.0)
+            shell = shell * shell
+            weights.append(jnp.concatenate(split2(shell * shell * (4.0 * t + 1.0)), axis=0))
+        outs = []
+        for u in range(UNROLL):
+            tile = tiles[u]
+            high = tile.astype(BF16).astype(F32)
+            low = tile - high
+            feats = jnp.concatenate(
+                [
+                    jnp.concatenate([jnp.where(left8, high, 0.0), jnp.where(left8, low, 0.0)], axis=0),
+                    jnp.concatenate([jnp.where(left8, 0.0, high), jnp.where(left8, 0.0, low)], axis=0),
+                ],
+                axis=0,
+            ).astype(BF16)
+            outs.append(
+                lax.dot_general(
+                    feats, weights[u], (((1,), (1,)), ((), ())), preferred_element_type=F32
+                )
+            )
+        for u in range(UNROLL):
+            ca, cb = ids[u]
+            got = outs[u]
+            acc_ref[ca] = acc_ref[ca] + (got[0:8] + got[8:16])
+            acc_ref[cb] = acc_ref[cb] + (got[16:24] + got[24:32])
         return carry
 
-    lax.fori_loop(0, recv_ref.shape[0], source, 0)
+    lax.fori_loop(0, (live + UNROLL - 1) // UNROLL, block, 0)
 
     def finish(a, carry):
         for p in range(PAIRS):
@@ -468,8 +566,9 @@
         + [pl.BlockSpec(memory_space=pltpu.VMEM)] * 3,
         out_specs=[pl.BlockSpec(memory_space=pltpu.VMEM)] * 2,
         scratch_shapes=[
-            pltpu.VMEM((CA * CB, 2, 64, 128), BF16),
+            pltpu.VMEM((CA * CB, 64, 128), BF16),
             pltpu.VMEM((CA * CB, 8, 128), F32),
+            pltpu.SMEM((recv.shape[0] * SLOTS // 2 + UNROLL + 8,), jnp.int32),
         ],
         compiler_params=pltpu.CompilerParams(vmem_limit_bytes=48 << 20),
         name="wall_terms",

time: 217 us -> 127 us (0.59)
  the two profiles are of different devices: /device:TPU:2 before, /device:TPU:99 now
where the time goes in v2:
time: 127 us; the launch traced here: 125 us
  Pallas kernels  70.9 us (56%)
  waiting for transfers between devices  26.1 us (21%)
  starting transfers between devices  19.2 us (15%)
  local copies, waits for them, and re-layouts  5.66 us (4%)
  other arithmetic  2.09 us (2%)
    pallas_call x1, Pallas kernels, near_terms(): pl.pallas_call(near_kernel, out_shape=jax.ShapeDtypeStruct((CA, PAIRS, 8,...  32.1 us
    pallas_call x1, Pallas kernels, wall_terms(): pl.pallas_call(wall_kernel, out_shape=(jax.ShapeDtypeStruct((CA, CB, 256)...  31.8 us
    ppermute x4, waiting for transfers between devices, shift_from(): return lax.ppermute(array, axis, pairs)  26.1 us
    all_to_all x1, starting transfers between devices, local(): lax.all_to_all(send, ('gx', 'gy'), split_axis=0, concat_axis=0, tiled=True)  10.1 us
    ppermute x4, starting transfers between devices, shift_from(): return lax.ppermute(array, axis, pairs)  9.09 us
    unnamed x11, local copies, waits for them, and re-layouts  4.53 us
    pallas_call x1, Pallas kernels, route_walls(): pl.pallas_call(lambda *refs: route_kernel(devices, *refs), out_shape=jax....  3.86 us
    pallas_call x1, Pallas kernels, pack_records(): pl.pallas_call(pack_kernel, out_shape=jax.ShapeDtypeStruct((CA, PAIRS, 16...  3.07 us
  transfers between devices with their start and end apart: 5, of which 3 were waited for; matrix products, arithmetic and copies ran while one was open for 2% of the time, Pallas kernels for 28%

profile of v2, /device:TPU:99, one launch (start us, length us, event | category | flops | bytes accessed | tf_op | source)
XLA Modules:
  0.0 124.7 jit_solution(16380426499129563385)
XLA Ops:
  0.6 0.0 copy-start.2
  0.6 1.0 copy-done.2
  1.7 0.0 copy-start.3
  1.7 0.7 copy-done.3
  2.4 0.0 copy-start.4
  2.4 0.7 copy-done.4
  3.0 3.9 %route_walls.1 = f32[128,40,128]{2,1,0:T(8,128)S(1)} custom-call(f32[256,512]{1,0:T(8,128)S(1)} %copy-done.2, s32[2,256]{1,0:T(2,128)S(1)} %bitcast.8, s32[2,256]{1,0:T(2,128)S(1)} %bitcast.9), custom_call_target="tpu_custom_call" | custom-call | tf_op jit(solution)/shard_map/route_walls/pallas_call | solution.py:151
  6.9 0.0 copy-start.1
  6.9 1.5 %copy-done.1 = f32[128,40,128]{2,1,0:T(8,128)} copy-done((f32[128,40,128]{2,1,0:T(8,128)}, f32[128,40,128]{2,1,0:T(8,128)S(1)}, u32[]{:S(2)}) %copy-start.1) | copy-done | bytes 2621464
  8.4 10.1 %all-to-all-start = ((f32[128,40,128]{2,1,0:T(8,128)}), f32[128,40,128]{2,1,0:T(8,128)S(1)}, u32[]{:S(2)}, u32[]{:S(2)}) async-start(f32[128,40,128]{2,1,0:T(8,128)} %copy-done.1), calls=%async_computation | async-start | bytes 5242880 | tf_op jit(solution)/shard_map/all_to_all | solution.py:595
  18.6 3.1 %pack_records.1.rec_ref = f32[16,4,16,128]{3,2,1,0:T(8,128)} custom-call(s32[8,16]{1,0:T(8,128)} %bitcast.11, f32[16,8,768]{2,1,0:T(8,128)} %fluid_ref.1), custom_call_target="tpu_custom_call" | custom-call | tf_op jit(solution)/shard_map/pack_records/pallas_call | solution.py:81
  21.7 0.0 copy-start
  21.7 1.0 fusion.1
  22.7 2.2 %collective-permute-start.1 = (f32[16,1,16,128]{3,2,1,0:T(8,128)S(1)}, f32[16,1,16,128]{3,2,1,0:T(8,128)S(1)}, u32[]{:S(2)}, u32[]{:S(2)}) collective-permute-start(f32[16,1,16,128]{3,2,1,0:T(8,128)S(1)} %get-tuple-element.9), channel_id=1, source_target_pairs={{1,0},{2,1},{3,2},{5,4},{6,5},{7,6},{9,8},{10,9},{11,10},{13,12},{... | collective-permute-start | bytes 393224 | tf_op jit(solution)/shard_map/ppermute | solution.py:582
  24.9 1.3 %collective-permute-start = (f32[16,1,16,128]{3,2,1,0:T(8,128)S(1)}, f32[16,1,16,128]{3,2,1,0:T(8,128)S(1)}, u32[]{:S(2)}, u32[]{:S(2)}) collective-permute-start(f32[16,1,16,128]{3,2,1,0:T(8,128)S(1)} %get-tuple-element.8), channel_id=1, source_target_pairs={{0,1},{1,2},{2,3},{4,5},{5,6},{6,7},{8,9},{9,10},{10,11},{12,13},{... | collective-permute-start | bytes 393224 | tf_op jit(solution)/shard_map/ppermute | solution.py:582
  26.2 22.4 %collective-permute-done.1 = f32[16,1,16,128]{3,2,1,0:T(8,128)S(1)} collective-permute-done((f32[16,1,16,128]{3,2,1,0:T(8,128)S(1)}, f32[16,1,16,128]{3,2,1,0:T(8,128)S(1)}, u32[]{:S(2)}, u32[]{:S(2)}) %collective-permute-start.1) | collective-permute-done | bytes 131104 | tf_op jit(solution)/shard_map/ppermute | solution.py:582
  48.7 1.7 %collective-permute-done = f32[16,1,16,128]{3,2,1,0:T(8,128)S(1)} collective-permute-done((f32[16,1,16,128]{3,2,1,0:T(8,128)S(1)}, f32[16,1,16,128]{3,2,1,0:T(8,128)S(1)}, u32[]{:S(2)}, u32[]{:S(2)}) %collective-permute-start) | collective-permute-done | bytes 131104 | tf_op jit(solution)/shard_map/ppermute | solution.py:582
  50.3 0.8 pad_maximum_fusion.3
  51.1 2.3 %collective-permute-start.3 = (f32[1,6,16,128]{3,2,1,0:T(8,128)S(1)}, f32[1,6,16,128]{3,2,1,0:T(8,128)S(1)}, u32[]{:S(2)}, u32[]{:S(2)}) collective-permute-start(f32[1,6,16,128]{3,2,1,0:T(8,128)S(1)} %get-tuple-element.7), channel_id=1, source_target_pairs={{4,0},{8,4},{12,8},{16,12},{20,16},{24,20},{28,24},{32,28},{36,32}... | collective-permute-start | bytes 147464 | tf_op jit(solution)/shard_map/ppermute | solution.py:582
  53.4 3.3 %collective-permute-start.2 = (f32[1,6,16,128]{3,2,1,0:T(8,128)S(1)}, f32[1,6,16,128]{3,2,1,0:T(8,128)S(1)}, u32[]{:S(2)}, u32[]{:S(2)}) collective-permute-start(f32[1,6,16,128]{3,2,1,0:T(8,128)S(1)} %get-tuple-element.6), channel_id=1, source_target_pairs={{0,4},{4,8},{8,12},{12,16},{16,20},{20,24},{24,28},{28,32},{32,36}... | collective-permute-start | bytes 147464 | tf_op jit(solution)/shard_map/ppermute | solution.py:582
  56.7 0.0 collective-permute-done.3
  56.7 2.0 %collective-permute-done.2 = f32[1,6,16,128]{3,2,1,0:T(8,128)S(1)} collective-permute-done((f32[1,6,16,128]{3,2,1,0:T(8,128)S(1)}, f32[1,6,16,128]{3,2,1,0:T(8,128)S(1)}, u32[]{:S(2)}, u32[]{:S(2)}) %collective-permute-start.2) | collective-permute-done | bytes 49184 | tf_op jit(solution)/shard_map/ppermute | solution.py:582
  58.7 1.1 pad_maximum_fusion.ext_ref
  59.8 32.1 %near_terms.1.near_ref = f32[16,4,8,128]{3,2,1,0:T(8,128)S(1)} custom-call(f32[18,6,16,128]{3,2,1,0:T(8,128)S(1)} %pad_maximum_fusion.ext_ref), custom_call_target="tpu_custom_call" | custom-call | tf_op jit(solution)/shard_map/near_terms/pallas_call | solution.py:409
  91.9 0.0 all-to-all-done.recv_ref
  92.0 0.2 fusion
  92.1 0.1 convert_element_type.8.cells_ref
  92.2 0.0 copy-done
  92.2 31.8 %wall_terms.1 = (f32[16,8,256]{2,1,0:T(8,128)}, f32[16,4,128]{2,1,0:T(4,128)S(1)}) custom-call(s32[2048]{0:T(1024)S(1)} %convert_element_type.8.cells_ref, f32[128,40,128]{2,1,0:T(8,128)S(1)} %all-to-all-done.recv_ref, f32[16,4,16,128]{3,2,1,0:T(8,128)S(1)} %copy-done, f32[16,4,8,128]{3,2,1,0:T(8,128)S(1)} %near_terms.1.near_ref), custom_call_target="tpu_custom_call" | custom-call | tf_op jit(solution)/shard_map/wall_terms/pallas_call | solution.py:559
  124.1 0.6 copy.9
Async XLA Ops:
  0.6 1.0 copy-start.2
  1.7 0.7 copy-start.3
  2.4 0.7 copy-start.4
  6.9 1.5 %copy-start.1 = (f32[128,40,128]{2,1,0:T(8,128)}, f32[128,40,128]{2,1,0:T(8,128)S(1)}, u32[]{:S(2)}) copy-start(f32[128,40,128]{2,1,0:T(8,128)S(1)} %route_walls.1) | copy-start | bytes 7864324
  8.4 83.5 %all-to-all-start = ((f32[128,40,128]{2,1,0:T(8,128)}), f32[128,40,128]{2,1,0:T(8,128)S(1)}, u32[]{:S(2)}, u32[]{:S(2)}) async-start(f32[128,40,128]{2,1,0:T(8,128)} %copy-done.1), calls=%async_computation | async-start | bytes 5242880 | tf_op jit(solution)/shard_map/all_to_all | solution.py:595
  21.7 70.6 %copy-start = (f32[16,4,16,128]{3,2,1,0:T(8,128)S(1)}, f32[16,4,16,128]{3,2,1,0:T(8,128)}, u32[]{:S(2)}) copy-start(f32[16,4,16,128]{3,2,1,0:T(8,128)} %pack_records.1.rec_ref) | copy-start | bytes 1572868
  22.7 25.9 %collective-permute-start.1 = (f32[16,1,16,128]{3,2,1,0:T(8,128)S(1)}, f32[16,1,16,128]{3,2,1,0:T(8,128)S(1)}, u32[]{:S(2)}, u32[]{:S(2)}) collective-permute-start(f32[16,1,16,128]{3,2,1,0:T(8,128)S(1)} %get-tuple-element.9), channel_id=1, source_target_pairs={{1,0},{2,1},{3,2},{5,4},{6,5},{7,6},{9,8},{10,9},{11,10},{13,12},{... | collective-permute-start | bytes 393224 | tf_op jit(solution)/shard_map/ppermute | solution.py:582
  24.9 25.4 %collective-permute-start = (f32[16,1,16,128]{3,2,1,0:T(8,128)S(1)}, f32[16,1,16,128]{3,2,1,0:T(8,128)S(1)}, u32[]{:S(2)}, u32[]{:S(2)}) collective-permute-start(f32[16,1,16,128]{3,2,1,0:T(8,128)S(1)} %get-tuple-element.8), channel_id=1, source_target_pairs={{0,1},{1,2},{2,3},{4,5},{5,6},{6,7},{8,9},{9,10},{10,11},{12,13},{... | collective-permute-start | bytes 393224 | tf_op jit(solution)/shard_map/ppermute | solution.py:582
  51.1 5.6 %collective-permute-start.3 = (f32[1,6,16,128]{3,2,1,0:T(8,128)S(1)}, f32[1,6,16,128]{3,2,1,0:T(8,128)S(1)}, u32[]{:S(2)}, u32[]{:S(2)}) collective-permute-start(f32[1,6,16,128]{3,2,1,0:T(8,128)S(1)} %get-tuple-element.7), channel_id=1, source_target_pairs={{4,0},{8,4},{12,8},{16,12},{20,16},{24,20},{28,24},{32,28},{36,32}... | collective-permute-start | bytes 147464 | tf_op jit(solution)/shard_map/ppermute | solution.py:582
  53.4 5.3 %collective-permute-start.2 = (f32[1,6,16,128]{3,2,1,0:T(8,128)S(1)}, f32[1,6,16,128]{3,2,1,0:T(8,128)S(1)}, u32[]{:S(2)}, u32[]{:S(2)}) collective-permute-start(f32[1,6,16,128]{3,2,1,0:T(8,128)S(1)} %get-tuple-element.6), channel_id=1, source_target_pairs={{0,4},{4,8},{8,12},{12,16},{16,20},{20,24},{24,28},{28,32},{32,36}... | collective-permute-start | bytes 147464 | tf_op jit(solution)/shard_map/ppermute | solution.py:582

commit v3 on v2

--- a/solution.py
+++ b/solution.py
@@ -180,7 +180,7 @@
 RIGHT_ORDER = ("hm", "hl", "mh")
 
 
-def near_kernel(
+def near_compute(
     ext_ref, out_ref, feat_ref, turn_ref, side_ref, geo_ref, sd0, mid0, mix0, sd1, mid1, mix1
 ):
     left1 = iota((1, 128), 1) < 64
@@ -405,13 +405,117 @@
     lax.fori_loop(0, CA * PAIRS // 2 + 1, step, 0)
 
 
-def near_terms(ext):
+def exchange_kernel(devices, rec_ref, send_ref, out_ref, recv_ref, ext_ref, *rest):
+    scratch, sems = rest[:-5], rest[-5:]
+    wall_send, wall_recv, own_sem, halo_send, halo_recv = sems
+    gx, gy = lax.axis_index("gx"), lax.axis_index("gy")
+    nx, ny = lax.axis_size("gx"), lax.axis_size("gy")
+    me = gx * ny + gy
+    barrier = pltpu.get_barrier_semaphore()
+
+    def greet(d, carry):
+        other = lax.rem(me + d, devices)
+        pl.semaphore_signal(
+            barrier,
+            inc=1,
+            device_id=(other // ny, lax.rem(other, ny)),
+            device_id_type=pl.DeviceIdType.MESH,
+        )
+        return carry
+
+    lax.fori_loop(1, devices, greet, 0)
+
+    own_copy = pltpu.make_async_copy(send_ref.at[me], recv_ref.at[me], own_sem)
+    own_copy.start()
+
+    def keep(a, carry):
+        for p in range(PAIRS):
+            ext_ref[a + 1, p + 1] = rec_ref[a, p]
+        return carry
+
+    lax.fori_loop(0, CA, keep, 0)
+    blank = jnp.zeros((16, 128), F32)
+
+    @pl.when(gx == 0)
+    def _():
+        for p in range(6):
+            ext_ref[0, p] = blank
+
+    @pl.when(gx == nx - 1)
+    def _():
+        for p in range(6):
+            ext_ref[CA + 1, p] = blank
+
+    @pl.when(gy == 0)
+    def _():
+        for a in range(CA + 2):
+            ext_ref[a, 0] = blank
+
+    @pl.when(gy == ny - 1)
+    def _():
+        for a in range(CA + 2):
+            ext_ref[a, PAIRS + 1] = blank
+
+    pl.semaphore_wait(barrier, devices - 1)
+
+    rows = {-1: (0, CA + 1), 1: (CA - 1, 0)}
+    cols = {-1: (0, PAIRS + 1), 1: (PAIRS - 1, 0)}
+    halos = []
+    for n, (dx, dy) in enumerate(
+        [(0, 1), (0, -1), (1, 0), (-1, 0), (1, 1), (1, -1), (-1, 1), (-1, -1)]
+    ):
+        src_a, dst_a = rows[dx] if dx else (pl.ds(0, CA), pl.ds(1, CA))
+        src_p, dst_p = cols[dy] if dy else (pl.ds(0, PAIRS), pl.ds(1, PAIRS))
+        to_x, to_y = gx + dx, gy + dy
+        sends = (to_x >= 0) & (to_x < nx) & (to_y >= 0) & (to_y < ny)
+        from_x, from_y = gx - dx, gy - dy
+        receives = (from_x >= 0) & (from_x < nx) & (from_y >= 0) & (from_y < ny)
+        copy = pltpu.make_async_remote_copy(
+            src_ref=rec_ref.at[src_a, src_p],
+            dst_ref=ext_ref.at[dst_a, dst_p],
+            send_sem=halo_send.at[n],
+            recv_sem=halo_recv.at[n],
+            device_id=(jnp.clip(to_x, 0, nx - 1), jnp.clip(to_y, 0, ny - 1)),
+            device_id_type=pl.DeviceIdType.MESH,
+        )
+        halos.append((sends, receives, copy))
+        pl.when(sends)(copy.start)
+
+    def post(d, carry):
+        other = lax.rem(me + d, devices)
+        pltpu.make_async_remote_copy(
+            src_ref=send_ref.at[other],
+            dst_ref=recv_ref.at[me],
+            send_sem=wall_send,
+            recv_sem=wall_recv,
+            device_id=(other // ny, lax.rem(other, ny)),
+            device_id_type=pl.DeviceIdType.MESH,
+        ).start()
+        return carry
+
+    lax.fori_loop(1, devices, post, 0)
+    for sends, receives, copy in halos:
+        pl.when(receives)(copy.wait_recv)
+    near_compute(ext_ref, out_ref, *scratch)
+    for sends, receives, copy in halos:
+        pl.when(sends)(copy.wait_send)
+    own_copy.wait()
+    everyone = recv_ref.at[pl.ds(0, devices - 1)]
+    pltpu.make_async_copy(everyone, everyone, wall_send).wait()
+    pltpu.make_async_copy(everyone, everyone, wall_recv).wait()
+
+
+def near_and_exchange(devices, records, send):
     return pl.pallas_call(
-        near_kernel,
-        out_shape=jax.ShapeDtypeStruct((CA, PAIRS, 8, 128), F32),
-        in_specs=[pl.BlockSpec(memory_space=pltpu.VMEM)],
-        out_specs=pl.BlockSpec(memory_space=pltpu.VMEM),
+        lambda *refs: exchange_kernel(devices, *refs),
+        out_shape=(
+            jax.ShapeDtypeStruct((CA, PAIRS, 8, 128), F32),
+            jax.ShapeDtypeStruct(send.shape, F32),
+        ),
+        in_specs=[pl.BlockSpec(memory_space=pltpu.VMEM), pl.BlockSpec(memory_space=pl.ANY)],
+        out_specs=[pl.BlockSpec(memory_space=pltpu.VMEM), pl.BlockSpec(memory_space=pl.ANY)],
         scratch_shapes=[
+            pltpu.VMEM((18, 6, 16, 128), F32),
             pltpu.VMEM((18, 6, 3, 64, 128), BF16),
             pltpu.VMEM((18, 6, 128, 128), BF16),
             pltpu.VMEM((18, PAIRS, 64, 128), BF16),
@@ -422,10 +526,19 @@
             pltpu.VMEM((3, 2, 256, 128), BF16),
             pltpu.VMEM((3, 2, 128, 128), BF16),
         ]
-        * 2,
-        compiler_params=pltpu.CompilerParams(vmem_limit_bytes=48 << 20),
-        name="near_terms",
-    )(ext)
+        * 2
+        + [
+            pltpu.SemaphoreType.DMA,
+            pltpu.SemaphoreType.DMA,
+            pltpu.SemaphoreType.DMA,
+            pltpu.SemaphoreType.DMA((8,)),
+            pltpu.SemaphoreType.DMA((8,)),
+        ],
+        compiler_params=pltpu.CompilerParams(
+            vmem_limit_bytes=40 << 20, collective_id=0, has_side_effects=True
+        ),
+        name="near_and_exchange",
+    )(records, send)
 
 
 UNROLL = 16
@@ -575,26 +688,12 @@
     )(cells, recv, records, near)
 
 
-def shift_from(array, axis, step):
-    peers = lax.axis_size(axis)
-    up = [(i, i + 1) for i in range(peers - 1)]
-    pairs = up if step > 0 else [(j, i) for i, j in up]
-    return lax.ppermute(array, axis, pairs)
-
-
 def local(fluid_state, cell_counts, wall_blocks, readers, targets):
     devices = lax.axis_size("gx") * lax.axis_size("gy")
     records = pack_records(fluid_state, cell_counts.T)
     send = route_walls(devices, wall_blocks, readers.T, targets.T)
-    before = shift_from(records[:, PAIRS - 1 :], "gy", 1)
-    after = shift_from(records[:, :1], "gy", -1)
-    wide = jnp.concatenate([before, records, after], axis=1)
-    above = shift_from(wide[CA - 1 :], "gx", 1)
-    below = shift_from(wide[:1], "gx", -1)
-    ext = jnp.concatenate([above, wide, below], axis=0)
-    recv = lax.all_to_all(send, ("gx", "gy"), split_axis=0, concat_axis=0, tiled=True)
+    near, recv = near_and_exchange(devices, records, send)
     cells = recv[:, 32, :16].astype(jnp.int32).reshape(-1)
-    near = near_terms(ext)
     rates, density = wall_terms(cells, recv, records, near)
     return (rates, density.reshape(CA, CB * 64))
 

time: 127 us -> 109 us (0.86); the launches traced: 125 us -> 109 us
  Pallas kernels: 70.9 us -> 105 us
  waiting for transfers between devices: 26.1 us -> 0 us
  starting transfers between devices: 19.2 us -> 0 us
  local copies, waits for them, and re-layouts: 5.66 us -> 3.1 us
  other arithmetic: 2.09 us -> 0.19 us
    pallas_call x1, Pallas kernels: 32.1 us -> 66.5 us  [near_and_exchange(): pl.pallas_call(lambda *refs: exchange_kernel(devices, *refs), out_shape=(...]
    ppermute x4 -> x0, waiting for transfers between devices: 26.1 us -> none  [shift_from(): return lax.ppermute(array, axis, pairs)]
    all_to_all x1 -> x0, starting transfers between devices: 10.1 us -> none  [local(): lax.all_to_all(send, ('gx', 'gy'), split_axis=0, concat_axis=0, tiled=True)]
    ppermute x4 -> x0, starting transfers between devices: 9.09 us -> none  [shift_from(): return lax.ppermute(array, axis, pairs)]
    unnamed x11 -> x9, local copies, waits for them, and re-layouts: 4.53 us -> 3.02 us
  transfers between devices with their start and end apart: 5 -> 0, of which waited for: 3 -> 0; matrix products, arithmetic and copies ran while one was open for 2% -> 0% of each run, Pallas kernels for 28% -> 0%
where the time goes in v3:
time: 109 us
  Pallas kernels  105 us (96%)
  local copies, waits for them, and re-layouts  3.1 us (3%)
    pallas_call x1, Pallas kernels, near_and_exchange(): pl.pallas_call(lambda *refs: exchange_kernel(devices, *refs), out_shape=(...  66.5 us
    pallas_call x1, Pallas kernels, wall_terms(): pl.pallas_call(wall_kernel, out_shape=(jax.ShapeDtypeStruct((CA, CB, 256)...  31.2 us
    pallas_call x1, Pallas kernels, route_walls(): pl.pallas_call(lambda *refs: route_kernel(devices, *refs), out_shape=jax....  3.85 us
    pallas_call x1, Pallas kernels, pack_records(): pl.pallas_call(pack_kernel, out_shape=jax.ShapeDtypeStruct((CA, PAIRS, 16...  3.05 us
    unnamed x9, local copies, waits for them, and re-layouts  3.02 us

profile of v3, /device:TPU:99, one launch (start us, length us, event | category | flops | bytes accessed | tf_op | source)
XLA Modules:
  0.0 108.6 jit_solution(10224593540216184049)
XLA Ops:
  0.6 3.1 %pack_records.1.refs_0_.rec_ref = f32[16,4,16,128]{3,2,1,0:T(8,128)} custom-call(s32[8,16]{1,0:T(8,128)} %bitcast.11, f32[16,8,768]{2,1,0:T(8,128)} %fluid_ref.1), custom_call_target="tpu_custom_call" | custom-call | tf_op jit(solution)/shard_map/pack_records/pallas_call | solution.py:81
  3.7 0.0 copy-start.1
  3.7 1.0 copy-done.1
  4.7 0.0 copy-start.2
  4.7 0.7 copy-done.2
  5.4 0.0 copy-start.3
  5.4 0.7 copy-done.3
  6.1 0.0 copy-start
  6.1 3.9 %route_walls.1.refs_1_ = f32[128,40,128]{2,1,0:T(8,128)S(1)} custom-call(f32[256,512]{1,0:T(8,128)S(1)} %copy-done.1, s32[2,256]{1,0:T(2,128)S(1)} %bitcast.8, s32[2,256]{1,0:T(2,128)S(1)} %bitcast.9), custom_call_target="tpu_custom_call" | custom-call | tf_op jit(solution)/shard_map/route_walls/pallas_call | solution.py:151
  10.0 0.0 copy-done
  10.0 66.5 %near_and_exchange.1 = (f32[16,4,8,128]{3,2,1,0:T(8,128)S(1)}, f32[128,40,128]{2,1,0:T(8,128)S(1)}) custom-call(f32[16,4,16,128]{3,2,1,0:T(8,128)S(1)} %copy-done, f32[128,40,128]{2,1,0:T(8,128)S(1)} %route_walls.1.refs_1_), custom_call_target="tpu_custom_call" | custom-call | tf_op jit(solution)/shard_map/near_and_exchange/pallas_call | solution.py:509
  76.5 0.2 convert_reduce_fusion
  76.7 0.1 convert_element_type.8.cells_ref
  76.8 31.2 %wall_terms.1 = (f32[16,8,256]{2,1,0:T(8,128)}, f32[16,4,128]{2,1,0:T(4,128)S(1)}) custom-call(s32[2048]{0:T(1024)S(1)} %convert_element_type.8.cells_ref, f32[128,40,128]{2,1,0:T(8,128)S(1)} %get-tuple-element.6.recv_ref, f32[16,4,16,128]{3,2,1,0:T(8,128)S(1)} %copy-done, f32[16,4,8,128]{3,2,1,0:T(8,128)S(1)} %get-tuple-element.7.near_ref), custom_call_target="tpu_custom_call" | custom-call | tf_op jit(solution)/shard_map/wall_terms/pallas_call | solution.py:672
  108.0 0.6 copy.9
Async XLA Ops:
  3.7 1.0 copy-start.1
  4.7 0.7 copy-start.2
  5.4 0.7 copy-start.3
  6.1 3.9 %copy-start = (f32[16,4,16,128]{3,2,1,0:T(8,128)S(1)}, f32[16,4,16,128]{3,2,1,0:T(8,128)}, u32[]{:S(2)}) copy-start(f32[16,4,16,128]{3,2,1,0:T(8,128)} %pack_records.1.refs_0_.rec_ref) | copy-start | bytes 1572868

commit v4 on v3

--- a/solution.py
+++ b/solution.py
@@ -11,6 +11,7 @@
 CB = 8
 PAIRS = 4
 SLOTS = 8
+SENDS = 8
 KERN_W = 21.0 / (16.0 * math.pi)
 KERN_F = 105.0 / (16.0 * math.pi)
 KAPPA = 0.02
@@ -38,7 +39,7 @@
     return high, middle, rest - middle
 
 
-def pack_kernel(counts_ref, fluid_ref, out_ref):
+def pack_records(counts_ref, fluid_ref, out_ref):
     lane = iota((8, 128), 1)
     left = lane < 64
     slot = lane - jnp.where(left, 0, 64)
@@ -77,20 +78,7 @@
     lax.fori_loop(0, CA, row, 0)
 
 
-def pack_records(fluid_state, counts_t):
-    return pl.pallas_call(
-        pack_kernel,
-        out_shape=jax.ShapeDtypeStruct((CA, PAIRS, 16, 128), F32),
-        in_specs=[
-            pl.BlockSpec(memory_space=pltpu.SMEM),
-            pl.BlockSpec(memory_space=pltpu.VMEM),
-        ],
-        out_specs=pl.BlockSpec(memory_space=pltpu.VMEM),
-        name="pack_records",
-    )(counts_t, fluid_state)
-
-
-def route_kernel(devices, wall_ref, readers_ref, targets_ref, out_ref, sel_ref, rhs_ref):
+def route_walls(devices, wall_ref, readers_ref, targets_ref, out_ref, sel_ref, rhs_ref):
     rows = wall_ref.shape[0]
     lane = iota((rows, 128), 1)
     left = lane < 64
@@ -142,24 +130,7 @@
             got = got.reshape(devices, SLOTS // 2, 128)
             for q in range(SLOTS // 2):
                 out_ref[:, q * 8 + 2 * v + odd, :] = got[:, q, :]
-    for k in range(8):
-        out_ref[:, 32 + k, :] = cells
-
-
-def route_walls(devices, wall_blocks, readers_t, targets_t):
-    rows = wall_blocks.shape[0]
-    return pl.pallas_call(
-        lambda *refs: route_kernel(devices, *refs),
-        out_shape=jax.ShapeDtypeStruct((devices, 40, 128), F32),
-        in_specs=[pl.BlockSpec(memory_space=pltpu.VMEM)] * 3,
-        out_specs=pl.BlockSpec(memory_space=pltpu.VMEM),
-        scratch_shapes=[
-            pltpu.VMEM((devices * SLOTS // 2, 2 * rows), BF16),
-            pltpu.VMEM((2 * rows, 384), BF16),
-        ],
-        compiler_params=pltpu.CompilerParams(vmem_limit_bytes=40 << 20),
-        name="route_walls",
-    )(wall_blocks, readers_t, targets_t)
+    out_ref[:, 32, :] = cells
 
 
 def stack_rows(row8, rows):
@@ -181,7 +152,7 @@
 
 
 def near_compute(
-    ext_ref, out_ref, feat_ref, turn_ref, side_ref, geo_ref, sd0, mid0, mix0, sd1, mid1, mix1
+    post, settle, ext_ref, out_ref, feat_ref, turn_ref, side_ref, geo_ref, sd0, mid0, mix0, sd1, mid1, mix1
 ):
     left1 = iota((1, 128), 1) < 64
     left8 = iota((8, 128), 1) < 64
@@ -231,11 +202,24 @@
         turn_ref[a, p] = jnp.concatenate([half, half], axis=0).T
 
     def prepare_row(a, carry):
-        for p in range(6):
-            prepare(a, p)
-        return carry
-
-    lax.fori_loop(0, 18, prepare_row, 0)
+        for p in range(PAIRS):
+            prepare(a + 1, p + 1)
+        for n in range(SENDS):
+            post(a * SENDS + n + 1)
+        return carry
+
+    lax.fori_loop(0, CA, prepare_row, 0)
+    settle()
+
+    def prepare_columns(a, carry):
+        for p in (0, PAIRS + 1):
+            prepare(a + 1, p)
+        return carry
+
+    lax.fori_loop(0, CA, prepare_columns, 0)
+    for p in range(PAIRS + 2):
+        prepare(0, p)
+        prepare(CA + 1, p)
 
     def sides(a, carry):
         for p in range(PAIRS):
@@ -405,12 +389,43 @@
     lax.fori_loop(0, CA * PAIRS // 2 + 1, step, 0)
 
 
-def exchange_kernel(devices, rec_ref, send_ref, out_ref, recv_ref, ext_ref, *rest):
-    scratch, sems = rest[:-5], rest[-5:]
-    wall_send, wall_recv, own_sem, halo_send, halo_recv = sems
+def exchange_kernel(
+    devices,
+    counts_ref,
+    fluid_hbm,
+    wall_hbm,
+    readers_hbm,
+    targets_hbm,
+    out_ref,
+    rec_ref,
+    recv_ref,
+    fluid_ref,
+    wall_ref,
+    readers_ref,
+    targets_ref,
+    send_ref,
+    sel_ref,
+    rhs_ref,
+    ext_ref,
+    *rest,
+):
+    scratch, (load_sem, wall_send, wall_recv, own_sem, halo_send, halo_recv) = rest[:-6], rest[-6:]
     gx, gy = lax.axis_index("gx"), lax.axis_index("gy")
     nx, ny = lax.axis_size("gx"), lax.axis_size("gy")
     me = gx * ny + gy
+    loads = [
+        pltpu.make_async_copy(src, dst, load_sem.at[n])
+        for n, (src, dst) in enumerate(
+            [
+                (readers_hbm, readers_ref),
+                (targets_hbm, targets_ref),
+                (wall_hbm, wall_ref),
+                (fluid_hbm, fluid_ref),
+            ]
+        )
+    ]
+    for load in loads:
+        load.start()
     barrier = pltpu.get_barrier_semaphore()
 
     def greet(d, carry):
@@ -424,16 +439,6 @@
         return carry
 
     lax.fori_loop(1, devices, greet, 0)
-
-    own_copy = pltpu.make_async_copy(send_ref.at[me], recv_ref.at[me], own_sem)
-    own_copy.start()
-
-    def keep(a, carry):
-        for p in range(PAIRS):
-            ext_ref[a + 1, p + 1] = rec_ref[a, p]
-        return carry
-
-    lax.fori_loop(0, CA, keep, 0)
     blank = jnp.zeros((16, 128), F32)
 
     @pl.when(gx == 0)
@@ -456,6 +461,18 @@
         for a in range(CA + 2):
             ext_ref[a, PAIRS + 1] = blank
 
+    for load in loads[:3]:
+        load.wait()
+    route_walls(devices, wall_ref, readers_ref, targets_ref, send_ref, sel_ref, rhs_ref)
+    loads[3].wait()
+    pack_records(counts_ref, fluid_ref, rec_ref)
+
+    def keep(a, carry):
+        for p in range(PAIRS):
+            ext_ref[a + 1, p + 1] = rec_ref[a, p]
+        return carry
+
+    lax.fori_loop(0, CA, keep, 0)
     pl.semaphore_wait(barrier, devices - 1)
 
     rows = {-1: (0, CA + 1), 1: (CA - 1, 0)}
@@ -481,40 +498,58 @@
         halos.append((sends, receives, copy))
         pl.when(sends)(copy.start)
 
-    def post(d, carry):
-        other = lax.rem(me + d, devices)
-        pltpu.make_async_remote_copy(
-            src_ref=send_ref.at[other],
-            dst_ref=recv_ref.at[me],
-            send_sem=wall_send,
-            recv_sem=wall_recv,
-            device_id=(other // ny, lax.rem(other, ny)),
-            device_id_type=pl.DeviceIdType.MESH,
-        ).start()
-        return carry
-
-    lax.fori_loop(1, devices, post, 0)
-    for sends, receives, copy in halos:
-        pl.when(receives)(copy.wait_recv)
-    near_compute(ext_ref, out_ref, *scratch)
+    used = pl.ds(0, 33)
+    own_copy = pltpu.make_async_copy(send_ref.at[me, used], recv_ref.at[me, used], own_sem)
+    own_copy.start()
+
+    def post(d):
+        other = lax.rem(me + d * 37, devices)
+
+        @pl.when(d < devices)
+        def _():
+            pltpu.make_async_remote_copy(
+                src_ref=send_ref.at[other, used],
+                dst_ref=recv_ref.at[me, used],
+                send_sem=wall_send,
+                recv_sem=wall_recv,
+                device_id=(other // ny, lax.rem(other, ny)),
+                device_id_type=pl.DeviceIdType.MESH,
+            ).start()
+
+    def settle():
+        for sends, receives, copy in halos:
+            pl.when(receives)(copy.wait_recv)
+
+    near_compute(post, settle, ext_ref, out_ref, *scratch)
     for sends, receives, copy in halos:
         pl.when(sends)(copy.wait_send)
     own_copy.wait()
-    everyone = recv_ref.at[pl.ds(0, devices - 1)]
+    everyone = recv_ref.at[pl.ds(0, devices - 1), used]
     pltpu.make_async_copy(everyone, everyone, wall_send).wait()
     pltpu.make_async_copy(everyone, everyone, wall_recv).wait()
 
 
-def near_and_exchange(devices, records, send):
+def near_and_exchange(devices, counts_t, fluid_state, wall_blocks, readers_t, targets_t):
+    walls = wall_blocks.shape[0]
+    vmem = pl.BlockSpec(memory_space=pltpu.VMEM)
+    anywhere = pl.BlockSpec(memory_space=pl.ANY)
     return pl.pallas_call(
         lambda *refs: exchange_kernel(devices, *refs),
         out_shape=(
             jax.ShapeDtypeStruct((CA, PAIRS, 8, 128), F32),
-            jax.ShapeDtypeStruct(send.shape, F32),
+            jax.ShapeDtypeStruct((CA, PAIRS, 16, 128), F32),
+            jax.ShapeDtypeStruct((devices, 40, 128), F32),
         ),
-        in_specs=[pl.BlockSpec(memory_space=pltpu.VMEM), pl.BlockSpec(memory_space=pl.ANY)],
-        out_specs=[pl.BlockSpec(memory_space=pltpu.VMEM), pl.BlockSpec(memory_space=pl.ANY)],
+        in_specs=[pl.BlockSpec(memory_space=pltpu.SMEM)] + [anywhere] * 4,
+        out_specs=[vmem, vmem, anywhere],
         scratch_shapes=[
+            pltpu.VMEM(fluid_state.shape, F32),
+            pltpu.VMEM(wall_blocks.shape, F32),
+            pltpu.VMEM(readers_t.shape, jnp.int32),
+            pltpu.VMEM(targets_t.shape, jnp.int32),
+            pltpu.VMEM((devices, 40, 128), F32),
+            pltpu.VMEM((devices * SLOTS // 2, 2 * walls), BF16),
+            pltpu.VMEM((2 * walls, 384), BF16),
             pltpu.VMEM((18, 6, 16, 128), F32),
             pltpu.VMEM((18, 6, 3, 64, 128), BF16),
             pltpu.VMEM((18, 6, 128, 128), BF16),
@@ -528,6 +563,7 @@
         ]
         * 2
         + [
+            pltpu.SemaphoreType.DMA((4,)),
             pltpu.SemaphoreType.DMA,
             pltpu.SemaphoreType.DMA,
             pltpu.SemaphoreType.DMA,
@@ -538,7 +574,7 @@
             vmem_limit_bytes=40 << 20, collective_id=0, has_side_effects=True
         ),
         name="near_and_exchange",
-    )(records, send)
+    )(counts_t, fluid_state, wall_blocks, readers_t, targets_t)
 
 
 UNROLL = 16
@@ -690,9 +726,9 @@
 
 def local(fluid_state, cell_counts, wall_blocks, readers, targets):
     devices = lax.axis_size("gx") * lax.axis_size("gy")
-    records = pack_records(fluid_state, cell_counts.T)
-    send = route_walls(devices, wall_blocks, readers.T, targets.T)
-    near, recv = near_and_exchange(devices, records, send)
+    near, records, recv = near_and_exchange(
+        devices, cell_counts.T, fluid_state, wall_blocks, readers.T, targets.T
+    )
     cells = recv[:, 32, :16].astype(jnp.int32).reshape(-1)
     rates, density = wall_terms(cells, recv, records, near)
     return (rates, density.reshape(CA, CB * 64))

time: 109 us -> 106 us (0.972)
  the two profiles are of different devices: /device:TPU:99 before, /device:TPU:15 now
where the time goes in v4:
time: 106 us
  Pallas kernels  101 us (95%)
  local copies, waits for them, and re-layouts  4.78 us (5%)
    pallas_call x1, Pallas kernels, near_and_exchange(): pl.pallas_call(lambda *refs: exchange_kernel(devices, *refs), out_shape=(...  68.7 us
    pallas_call x1, Pallas kernels, wall_terms(): pl.pallas_call(wall_kernel, out_shape=(jax.ShapeDtypeStruct((CA, CB, 256)...  31.8 us
    unnamed x11, local copies, waits for them, and re-layouts  4.7 us

profile of v4, /device:TPU:15, one launch (start us, length us, event | category | flops | bytes accessed | tf_op | source)
XLA Modules:
  0.0 106.2 jit_solution(10947791608170095552)
XLA Ops:
  0.6 0.0 copy-start
  0.6 1.0 copy-done
  1.7 0.0 copy-start.1
  1.7 1.0 copy-done.1
  2.7 0.0 copy-start.2
  2.7 0.7 copy-done.2
  3.4 0.0 copy-start.3
  3.4 0.7 copy-done.3
  4.0 0.0 copy-start.4
  4.0 0.7 copy-done.4
  4.7 68.7 %near_and_exchange.1 = (f32[16,4,8,128]{3,2,1,0:T(8,128)S(1)}, f32[16,4,16,128]{3,2,1,0:T(8,128)S(1)}, f32[128,40,128]{2,1,0:T(8,128)S(1)}) custom-call(s32[8,16]{1,0:T(8,128)S(1)} %bitcast.8, f32[16,8,768]{2,1,0:T(8,128)S(1)} %copy-done.1, f32[256,512]{1,0:T(8,128)S(1)} %copy-done, s32[2,256]{1,0:T(2,128)S(1)} %bitcast.9, s32[2,256]{1,0:T(2,128)S(1)} %bitcast.10), custom_call_target="tpu_custom_call" | custom-call | tf_op jit(solution)/shard_map/near_and_exchange/pallas_call | solution.py:536
  73.4 0.2 convert_reduce_fusion
  73.6 0.1 convert_element_type.8.cells_ref
  73.7 31.8 %wall_terms.1 = (f32[16,8,256]{2,1,0:T(8,128)}, f32[16,4,128]{2,1,0:T(4,128)S(1)}) custom-call(s32[2048]{0:T(1024)S(1)} %convert_element_type.8.cells_ref, f32[128,40,128]{2,1,0:T(8,128)S(1)} %get-tuple-element.7.recv_ref, f32[16,4,16,128]{3,2,1,0:T(8,128)S(1)} %get-tuple-element.8.rec_ref, f32[16,4,8,128]{3,2,1,0:T(8,128)S(1)} %get-tuple-element.9.near_ref), custom_call_target="tpu_custom_call" | custom-call | tf_op jit(solution)/shard_map/wall_terms/pallas_call | solution.py:708
  105.5 0.6 copy.9
Async XLA Ops:
  0.6 1.0 copy-start
  1.7 1.0 copy-start.1
  2.7 0.7 copy-start.2
  3.4 0.7 copy-start.3
  4.0 0.7 copy-start.4

commit v5 on v4

--- a/solution.py
+++ b/solution.py
@@ -11,7 +11,8 @@
 CB = 8
 PAIRS = 4
 SLOTS = 8
-SENDS = 8
+SENDS = 1
+STEP_SENDS = 2
 KERN_W = 21.0 / (16.0 * math.pi)
 KERN_F = 105.0 / (16.0 * math.pi)
 KAPPA = 0.02
@@ -39,7 +40,7 @@
     return high, middle, rest - middle
 
 
-def pack_records(counts_ref, fluid_ref, out_ref):
+def pack_records(counts_ref, fluid_ref, out_ref, greet):
     lane = iota((8, 128), 1)
     left = lane < 64
     slot = lane - jnp.where(left, 0, 64)
@@ -73,6 +74,8 @@
                     line = jnp.where(slot[:1] < count, line, 0.0)
                 out_ref[a, p, c : c + 1, :] = line
             out_ref[a, p, 13:16, :] = jnp.zeros((3, 128), F32)
+        for n in range(SLOTS):
+            greet(a * SLOTS + n + 1)
         return carry
 
     lax.fori_loop(0, CA, row, 0)
@@ -152,7 +155,7 @@
 
 
 def near_compute(
-    post, settle, ext_ref, out_ref, feat_ref, turn_ref, side_ref, geo_ref, sd0, mid0, mix0, sd1, mid1, mix1
+    post, settle, ext_ref, out_ref, lhs_ref, feat_ref, turn_ref, side_ref, geo_ref, sd0, mid0, mix0, sd1, mid1, mix1
 ):
     left1 = iota((1, 128), 1) < 64
     left8 = iota((8, 128), 1) < 64
@@ -369,6 +372,24 @@
         for n, line in enumerate((density, ax, ay, az, heat)):
             out_ref[a, p, n : n + 1, :] = line
 
+    def wall_side(k):
+        a = k // PAIRS
+        p = k - a * PAIRS
+        row = lambda c: ext_ref[a + 1, p + 1, c : c + 1, :]
+        x = row(0) - 0.5
+        y = row(1) - 0.5
+        z = row(2) - 2.0
+        h = row(10)
+        s = 0.25 / (h * h)
+        norm = x * x + y * y + z * z
+        rows = s * stack_rows(
+            row8, [-2.0 * x, -2.0 * y, -2.0 * z, jnp.ones_like(x), norm, jnp.zeros_like(x)]
+        )
+        half = jnp.concatenate(groups(*split3(rows), LEFT_ORDER) + [zero16], axis=0)
+        both = jnp.concatenate([half, half], axis=0).T
+        lhs_ref[2 * k] = both[:64]
+        lhs_ref[2 * k + 1] = both[64:]
+
     last = CA * PAIRS - 1
     slots = ((sd0, mid0, mix0), (sd1, mid1, mix1))
     for _, mid_ref, mix_ref in slots:
@@ -384,6 +405,9 @@
             gather(jnp.clip(k - 1, 0, last), mid_last, mix_last)
             distances(jnp.minimum(k + 1, last), sd_next)
             weigh(sd_ref, mid_ref, mix_ref)
+            wall_side(jnp.minimum(k, last))
+            for n in range(STEP_SENDS):
+                post(CA * SENDS + k * STEP_SENDS + n + 1)
         return carry
 
     lax.fori_loop(0, CA * PAIRS // 2 + 1, step, 0)
@@ -398,7 +422,9 @@
     targets_hbm,
     out_ref,
     rec_ref,
+    lhs_hbm,
     recv_ref,
+    lhs_ref,
     fluid_ref,
     wall_ref,
     readers_ref,
@@ -424,21 +450,22 @@
             ]
         )
     ]
-    for load in loads:
+    for load in loads[::-1]:
         load.start()
     barrier = pltpu.get_barrier_semaphore()
 
-    def greet(d, carry):
+    def greet(d):
         other = lax.rem(me + d, devices)
-        pl.semaphore_signal(
-            barrier,
-            inc=1,
-            device_id=(other // ny, lax.rem(other, ny)),
-            device_id_type=pl.DeviceIdType.MESH,
-        )
-        return carry
-
-    lax.fori_loop(1, devices, greet, 0)
+
+        @pl.when(d < devices)
+        def _():
+            pl.semaphore_signal(
+                barrier,
+                inc=1,
+                device_id=(other // ny, lax.rem(other, ny)),
+                device_id_type=pl.DeviceIdType.MESH,
+            )
+
     blank = jnp.zeros((16, 128), F32)
 
     @pl.when(gx == 0)
@@ -461,11 +488,11 @@
         for a in range(CA + 2):
             ext_ref[a, PAIRS + 1] = blank
 
+    loads[3].wait()
+    pack_records(counts_ref, fluid_ref, rec_ref, greet)
     for load in loads[:3]:
         load.wait()
     route_walls(devices, wall_ref, readers_ref, targets_ref, send_ref, sel_ref, rhs_ref)
-    loads[3].wait()
-    pack_records(counts_ref, fluid_ref, rec_ref)
 
     def keep(a, carry):
         for p in range(PAIRS):
@@ -520,29 +547,35 @@
         for sends, receives, copy in halos:
             pl.when(receives)(copy.wait_recv)
 
-    near_compute(post, settle, ext_ref, out_ref, *scratch)
+    near_compute(post, settle, ext_ref, out_ref, lhs_ref, *scratch)
+    leave = pltpu.make_async_copy(lhs_ref, lhs_hbm, load_sem.at[0])
+    leave.start()
     for sends, receives, copy in halos:
         pl.when(sends)(copy.wait_send)
     own_copy.wait()
     everyone = recv_ref.at[pl.ds(0, devices - 1), used]
     pltpu.make_async_copy(everyone, everyone, wall_send).wait()
     pltpu.make_async_copy(everyone, everyone, wall_recv).wait()
+    leave.wait()
 
 
 def near_and_exchange(devices, counts_t, fluid_state, wall_blocks, readers_t, targets_t):
     walls = wall_blocks.shape[0]
     vmem = pl.BlockSpec(memory_space=pltpu.VMEM)
     anywhere = pl.BlockSpec(memory_space=pl.ANY)
+    hbm = pl.BlockSpec(memory_space=pltpu.HBM)
     return pl.pallas_call(
         lambda *refs: exchange_kernel(devices, *refs),
         out_shape=(
             jax.ShapeDtypeStruct((CA, PAIRS, 8, 128), F32),
             jax.ShapeDtypeStruct((CA, PAIRS, 16, 128), F32),
+            jax.ShapeDtypeStruct((CA * CB, 64, 128), BF16),
             jax.ShapeDtypeStruct((devices, 40, 128), F32),
         ),
-        in_specs=[pl.BlockSpec(memory_space=pltpu.SMEM)] + [anywhere] * 4,
-        out_specs=[vmem, vmem, anywhere],
+        in_specs=[pl.BlockSpec(memory_space=pltpu.SMEM)] + [hbm] * 4,
+        out_specs=[vmem, vmem, anywhere, anywhere],
         scratch_shapes=[
+            pltpu.VMEM((CA * CB, 64, 128), BF16),
             pltpu.VMEM(fluid_state.shape, F32),
             pltpu.VMEM(wall_blocks.shape, F32),
             pltpu.VMEM(readers_t.shape, jnp.int32),
@@ -571,16 +604,41 @@
             pltpu.SemaphoreType.DMA((8,)),
         ],
         compiler_params=pltpu.CompilerParams(
-            vmem_limit_bytes=40 << 20, collective_id=0, has_side_effects=True
+            vmem_limit_bytes=26 << 20, collective_id=0, has_side_effects=True
         ),
         name="near_and_exchange",
-    )(counts_t, fluid_state, wall_blocks, readers_t, targets_t)
+    )(
+        counts_t,
+        *[
+            pltpu.with_memory_space_constraint(array, pltpu.HBM)
+            for array in (fluid_state, wall_blocks, readers_t, targets_t)
+        ],
+    )
 
 
 UNROLL = 16
 
 
-def wall_kernel(cells_ref, recv_ref, rec_ref, near_ref, rates_ref, dens_ref, lhs_ref, acc_ref, list_ref):
+def wall_kernel(
+    recv_ref,
+    rec_ref,
+    near_ref,
+    lhs_hbm,
+    rates_ref,
+    dens_ref,
+    lhs_ref,
+    acc_ref,
+    turn_ref,
+    cells_ref,
+    list_ref,
+    sems,
+):
+    enter = pltpu.make_async_copy(lhs_hbm, lhs_ref, sems.at[0])
+    enter.start()
+    turn_ref[...] = recv_ref[:, 32, :].astype(jnp.int32)
+    spread = pltpu.make_async_copy(turn_ref, cells_ref, sems.at[1])
+    spread.start()
+    spread.wait()
     lane1 = iota((1, 128), 1)
     left1 = lane1 < 64
     row8 = iota((8, 128), 0)
@@ -591,35 +649,20 @@
     def listing(src, m):
         for q in range(SLOTS // 2):
             list_ref[m + q] = src * (SLOTS // 2) + q
-        return m + (cells_ref[src * 16 + SLOTS] + 1) // 2
-
-    live = lax.fori_loop(0, recv_ref.shape[0], listing, 0)
+        return m + (cells_ref[src, SLOTS] + 1) // 2
+
+    def clear(a, m):
+        for n in range(CB):
+            acc_ref[a * CB + n] = zero8
+        for n in range(recv_ref.shape[0] // CA):
+            m = listing(a * (recv_ref.shape[0] // CA) + n, m)
+        return m
+
+    live = lax.fori_loop(0, CA, clear, 0)
     for q in range(UNROLL):
         list_ref[live + q] = 0
 
-    def cell_features(k, carry):
-        a = k // PAIRS
-        p = k - a * PAIRS
-        row = lambda c: rec_ref[a, p, c : c + 1, :]
-        x = row(0) - 0.5
-        y = row(1) - 0.5
-        z = row(2) - 2.0
-        h = row(10)
-        s = 0.25 / (h * h)
-        norm = x * x + y * y + z * z
-        rows = s * stack_rows(
-            row8, [-2.0 * x, -2.0 * y, -2.0 * z, jnp.ones_like(x), norm, jnp.zeros_like(x)]
-        )
-        half = jnp.concatenate(groups(*split3(rows), LEFT_ORDER) + [zero16], axis=0)
-        both = jnp.concatenate([half, half], axis=0).T
-        lhs_ref[2 * k] = both[:64]
-        lhs_ref[2 * k + 1] = both[64:]
-        acc_ref[2 * k] = zero8
-        acc_ref[2 * k + 1] = zero8
-        return carry
-
-    lax.fori_loop(0, CA * PAIRS, cell_features, 0)
-
+    enter.wait()
     center = jnp.where(row8 == 2, 2.0, jnp.where(row8 < 2, 0.5, 0.0))
 
     def block(k, carry):
@@ -629,8 +672,8 @@
             pair = list_ref[at]
             src = pair // (SLOTS // 2)
             q = pair - src * (SLOTS // 2)
-            ca = cells_ref[src * 16 + 2 * q]
-            cb = cells_ref[src * 16 + 2 * q + 1]
+            ca = cells_ref[src, 2 * q]
+            cb = cells_ref[src, 2 * q + 1]
             ids.append((ca, cb))
             tile = recv_ref[src, pl.ds(pl.multiple_of(q * 8, 8), 8), :]
             tiles.append(jnp.where(at < live, tile, 0.0))
@@ -653,7 +696,7 @@
             shell = jnp.maximum(1.0 - t, 0.0)
             shell = shell * shell
             weights.append(jnp.concatenate(split2(shell * shell * (4.0 * t + 1.0)), axis=0))
-        outs = []
+        outs, lines = [], []
         for u in range(UNROLL):
             tile = tiles[u]
             high = tile.astype(BF16).astype(F32)
@@ -665,11 +708,19 @@
                 ],
                 axis=0,
             ).astype(BF16)
-            outs.append(
-                lax.dot_general(
-                    feats, weights[u], (((1,), (1,)), ((), ())), preferred_element_type=F32
+            blank = jnp.zeros((32, 128), BF16)
+            lines.append(
+                jnp.concatenate([blank, feats] if u % 2 else [feats, blank], axis=1)
+            )
+            if u % 2:
+                got = lax.dot_general(
+                    jnp.concatenate(lines, axis=0),
+                    jnp.concatenate([weights[u - 1], weights[u]], axis=1),
+                    (((1,), (1,)), ((), ())),
+                    preferred_element_type=F32,
                 )
-            )
+                outs += [got[0:32], got[32:64]]
+                lines = []
         for u in range(UNROLL):
             ca, cb = ids[u]
             got = outs[u]
@@ -704,33 +755,35 @@
     lax.fori_loop(0, CA, finish, 0)
 
 
-def wall_terms(cells, recv, records, near):
+def wall_terms(recv, records, near, sides):
     return pl.pallas_call(
         wall_kernel,
         out_shape=(
             jax.ShapeDtypeStruct((CA, CB, 256), F32),
             jax.ShapeDtypeStruct((CA, PAIRS, 128), F32),
         ),
-        in_specs=[pl.BlockSpec(memory_space=pltpu.SMEM)]
-        + [pl.BlockSpec(memory_space=pltpu.VMEM)] * 3,
+        in_specs=[pl.BlockSpec(memory_space=pltpu.VMEM)] * 3
+        + [pl.BlockSpec(memory_space=pl.ANY)],
         out_specs=[pl.BlockSpec(memory_space=pltpu.VMEM)] * 2,
         scratch_shapes=[
             pltpu.VMEM((CA * CB, 64, 128), BF16),
             pltpu.VMEM((CA * CB, 8, 128), F32),
+            pltpu.VMEM((recv.shape[0], 128), jnp.int32),
+            pltpu.SMEM((recv.shape[0], 128), jnp.int32),
             pltpu.SMEM((recv.shape[0] * SLOTS // 2 + UNROLL + 8,), jnp.int32),
+            pltpu.SemaphoreType.DMA((2,)),
         ],
-        compiler_params=pltpu.CompilerParams(vmem_limit_bytes=48 << 20),
+        compiler_params=pltpu.CompilerParams(vmem_limit_bytes=10 << 20),
         name="wall_terms",
-    )(cells, recv, records, near)
+    )(recv, records, near, sides)
 
 
 def local(fluid_state, cell_counts, wall_blocks, readers, targets):
     devices = lax.axis_size("gx") * lax.axis_size("gy")
-    near, records, recv = near_and_exchange(
+    near, records, sides, recv = near_and_exchange(
         devices, cell_counts.T, fluid_state, wall_blocks, readers.T, targets.T
     )
-    cells = recv[:, 32, :16].astype(jnp.int32).reshape(-1)
-    rates, density = wall_terms(cells, recv, records, near)
+    rates, density = wall_terms(recv, records, near, sides)
     return (rates, density.reshape(CA, CB * 64))
 
 

time: 106 us -> 81.9 us (0.77)
  the two profiles are of different devices: /device:TPU:15 before, /device:TPU:0 now
where the time goes in v5:
time: 81.9 us; the launch traced here: 81.7 us
  Pallas kernels  79.8 us (97%)
  local copies, waits for them, and re-layouts  1.3 us (2%)
    pallas_call x1, Pallas kernels, near_and_exchange(): pl.pallas_call(lambda *refs: exchange_kernel(devices, *refs), out_shape=(...  54.7 us
    pallas_call x1, Pallas kernels, wall_terms(): pl.pallas_call(wall_kernel, out_shape=(jax.ShapeDtypeStruct((CA, CB, 256)...  25.1 us

profile of v5, /device:TPU:0, one launch (start us, length us, event | category | flops | bytes accessed | tf_op | source)
XLA Modules:
  0.0 81.7 jit_solution(13273165241636629703)
XLA Ops:
  0.6 0.0 copy-start
  0.6 0.7 copy-done
  1.3 54.7 %near_and_exchange.1 = (f32[16,4,8,128]{3,2,1,0:T(8,128)S(1)}, f32[16,4,16,128]{3,2,1,0:T(8,128)S(1)}, bf16[128,64,128]{2,1,0:T(8,128)(2,1)S(1)}, f32[128,40,128]{2,1,0:T(8,128)S(1)}) custom-call(s32[8,16]{1,0:T(8,128)S(1)} %bitcast.8, f32[16,8,768]{2,1,0:T(8,128)} %refs_1_.1, f32[256,512]{1,0:T(8,128)} %refs_2_.1, s32[2,256]{1,0:T(2,128)} %bitcast.10, ...), custom_call_target="tpu_custom_call" | custom-call | tf_op jit(solution)/shard_map/near_and_exchange/pallas_call | solution.py:567
  56.0 25.1 %wall_terms.1 = (f32[16,8,256]{2,1,0:T(8,128)}, f32[16,4,128]{2,1,0:T(4,128)S(1)}) custom-call(f32[128,40,128]{2,1,0:T(8,128)S(1)} %get-tuple-element.8.recv_ref, f32[16,4,16,128]{3,2,1,0:T(8,128)S(1)} %get-tuple-element.9.rec_ref, f32[16,4,8,128]{3,2,1,0:T(8,128)S(1)} %get-tuple-element.10.near_ref, bf16[128,64,128]{2,1,0:T(8,128)(2,1)S(1)} %get-tuple-element.11.lhs_hbm), custom_call_target="tpu_custom_call" | custom-call | tf_op jit(solution)/shard_map/wall_terms/pallas_call | solution.py:759
  81.1 0.6 copy.9
Async XLA Ops:
  0.6 0.7 copy-start

commit v6 on v5

--- a/solution.py
+++ b/solution.py
@@ -155,7 +155,7 @@
 
 
 def near_compute(
-    post, settle, ext_ref, out_ref, lhs_ref, feat_ref, turn_ref, side_ref, geo_ref, sd0, mid0, mix0, sd1, mid1, mix1
+    post, settle, ext_ref, out_ref, side_out, feat_ref, turn_ref, side_ref, geo_ref, sd0, mid0, mix0, sd1, mid1, mix1
 ):
     left1 = iota((1, 128), 1) < 64
     left8 = iota((8, 128), 1) < 64
@@ -385,10 +385,12 @@
         rows = s * stack_rows(
             row8, [-2.0 * x, -2.0 * y, -2.0 * z, jnp.ones_like(x), norm, jnp.zeros_like(x)]
         )
-        half = jnp.concatenate(groups(*split3(rows), LEFT_ORDER) + [zero16], axis=0)
-        both = jnp.concatenate([half, half], axis=0).T
-        lhs_ref[2 * k] = both[:64]
-        lhs_ref[2 * k + 1] = both[64:]
+        here, there = split3(rows), split3(pltpu.roll(rows, 64, 1))
+        for n, side, parts in ((0, 0, here), (0, 1, there), (1, 0, there), (1, 1, here)):
+            kept = [jnp.where(left8, 0.0, t) if side else jnp.where(left8, t, 0.0) for t in parts]
+            side_out[2 * k + n, side] = jnp.concatenate(
+                groups(*kept, RIGHT_ORDER) + [zero16], axis=0
+            )
 
     last = CA * PAIRS - 1
     slots = ((sd0, mid0, mix0), (sd1, mid1, mix1))
@@ -410,7 +412,8 @@
                 post(CA * SENDS + k * STEP_SENDS + n + 1)
         return carry
 
-    lax.fori_loop(0, CA * PAIRS // 2 + 1, step, 0)
+    lax.fori_loop(0, CA * PAIRS // 2, step, 0)
+    gather(last, mid1, mix1)
 
 
 def exchange_kernel(
@@ -422,9 +425,8 @@
     targets_hbm,
     out_ref,
     rec_ref,
-    lhs_hbm,
+    side_out,
     recv_ref,
-    lhs_ref,
     fluid_ref,
     wall_ref,
     readers_ref,
@@ -547,16 +549,13 @@
         for sends, receives, copy in halos:
             pl.when(receives)(copy.wait_recv)
 
-    near_compute(post, settle, ext_ref, out_ref, lhs_ref, *scratch)
-    leave = pltpu.make_async_copy(lhs_ref, lhs_hbm, load_sem.at[0])
-    leave.start()
+    near_compute(post, settle, ext_ref, out_ref, side_out, *scratch)
     for sends, receives, copy in halos:
         pl.when(sends)(copy.wait_send)
     own_copy.wait()
     everyone = recv_ref.at[pl.ds(0, devices - 1), used]
     pltpu.make_async_copy(everyone, everyone, wall_send).wait()
     pltpu.make_async_copy(everyone, everyone, wall_recv).wait()
-    leave.wait()
 
 
 def near_and_exchange(devices, counts_t, fluid_state, wall_blocks, readers_t, targets_t):
@@ -569,13 +568,12 @@
         out_shape=(
             jax.ShapeDtypeStruct((CA, PAIRS, 8, 128), F32),
             jax.ShapeDtypeStruct((CA, PAIRS, 16, 128), F32),
-            jax.ShapeDtypeStruct((CA * CB, 64, 128), BF16),
+            jax.ShapeDtypeStruct((CA * CB, 2, 64, 128), BF16),
             jax.ShapeDtypeStruct((devices, 40, 128), F32),
         ),
         in_specs=[pl.BlockSpec(memory_space=pltpu.SMEM)] + [hbm] * 4,
-        out_specs=[vmem, vmem, anywhere, anywhere],
+        out_specs=[vmem, vmem, vmem, anywhere],
         scratch_shapes=[
-            pltpu.VMEM((CA * CB, 64, 128), BF16),
             pltpu.VMEM(fluid_state.shape, F32),
             pltpu.VMEM(wall_blocks.shape, F32),
             pltpu.VMEM(readers_t.shape, jnp.int32),
@@ -616,27 +614,24 @@
     )
 
 
-UNROLL = 16
+UNROLL = 32
 
 
 def wall_kernel(
     recv_ref,
     rec_ref,
     near_ref,
-    lhs_hbm,
+    side_ref,
     rates_ref,
     dens_ref,
-    lhs_ref,
     acc_ref,
     turn_ref,
     cells_ref,
     list_ref,
     sems,
 ):
-    enter = pltpu.make_async_copy(lhs_hbm, lhs_ref, sems.at[0])
-    enter.start()
-    turn_ref[...] = recv_ref[:, 32, :].astype(jnp.int32)
-    spread = pltpu.make_async_copy(turn_ref, cells_ref, sems.at[1])
+    turn_ref[...] = recv_ref[:, 32, :].T[0:16].astype(jnp.int32)
+    spread = pltpu.make_async_copy(turn_ref, cells_ref, sems.at[0])
     spread.start()
     spread.wait()
     lane1 = iota((1, 128), 1)
@@ -649,11 +644,12 @@
     def listing(src, m):
         for q in range(SLOTS // 2):
             list_ref[m + q] = src * (SLOTS // 2) + q
-        return m + (cells_ref[src, SLOTS] + 1) // 2
+        return m + (cells_ref[SLOTS, src] + 1) // 2
 
     def clear(a, m):
         for n in range(CB):
-            acc_ref[a * CB + n] = zero8
+            acc_ref[0, a * CB + n] = zero8
+            acc_ref[1, a * CB + n] = zero8
         for n in range(recv_ref.shape[0] // CA):
             m = listing(a * (recv_ref.shape[0] // CA) + n, m)
         return m
@@ -662,7 +658,6 @@
     for q in range(UNROLL):
         list_ref[live + q] = 0
 
-    enter.wait()
     center = jnp.where(row8 == 2, 2.0, jnp.where(row8 < 2, 0.5, 0.0))
 
     def block(k, carry):
@@ -672,69 +667,72 @@
             pair = list_ref[at]
             src = pair // (SLOTS // 2)
             q = pair - src * (SLOTS // 2)
-            ca = cells_ref[src, 2 * q]
-            cb = cells_ref[src, 2 * q + 1]
-            ids.append((ca, cb))
+            ids.append((cells_ref[2 * q, src], cells_ref[2 * q + 1, src]))
             tile = recv_ref[src, pl.ds(pl.multiple_of(q * 8, 8), 8), :]
             tiles.append(jnp.where(at < live, tile, 0.0))
-            c = tile - center
-            sq = c * c
-            norm = sq[0:1] + sq[1:2] + sq[2:3]
-            rows = jnp.where(
-                row8 < 3, c, jnp.where(row8 == 3, norm, jnp.where(row8 == 4, 1.0, 0.0))
-            )
-            parts = split3(rows)
-            lefts = groups(*[jnp.where(left8, t, 0.0) for t in parts], RIGHT_ORDER) + [zero16]
-            rights = groups(*[jnp.where(left8, 0.0, t) for t in parts], RIGHT_ORDER) + [zero16]
-            right = jnp.concatenate(lefts + rights, axis=0)
-            lhs = jnp.concatenate([lhs_ref[ca][:, 0:64], lhs_ref[cb][:, 64:128]], axis=1)
-            squares.append(jnp.dot(lhs, right, preferred_element_type=F32))
+        for u in range(0, UNROLL, 2):
+            stacks = []
+            for tile in tiles[u : u + 2]:
+                c = tile - center
+                sq = c * c
+                norm = sq[0:1] + sq[1:2] + sq[2:3]
+                rows = jnp.where(
+                    row8 < 3, c, jnp.where(row8 == 3, norm, jnp.where(row8 == 4, 1.0, 0.0))
+                )
+                stacks += groups(*split3(rows), LEFT_ORDER) + [zero16]
+            turned = jnp.concatenate(stacks, axis=0).T
+            for side in range(2):
+                right = jnp.concatenate(
+                    [side_ref[ids[u][side], 0], side_ref[ids[u + 1][side], 1]], axis=0
+                )
+                squares.append(
+                    jnp.dot(
+                        turned[64 * side : 64 * side + 64], right, preferred_element_type=F32
+                    )
+                )
         weights = []
-        for u in range(UNROLL):
-            q2 = jnp.maximum(squares[u], 1e-20)
+        for q2 in squares:
+            q2 = jnp.maximum(q2, 1e-20)
             t = q2 * lax.rsqrt(q2)
             shell = jnp.maximum(1.0 - t, 0.0)
             shell = shell * shell
             weights.append(jnp.concatenate(split2(shell * shell * (4.0 * t + 1.0)), axis=0))
-        outs, lines = [], []
-        for u in range(UNROLL):
-            tile = tiles[u]
-            high = tile.astype(BF16).astype(F32)
-            low = tile - high
-            feats = jnp.concatenate(
-                [
-                    jnp.concatenate([jnp.where(left8, high, 0.0), jnp.where(left8, low, 0.0)], axis=0),
-                    jnp.concatenate([jnp.where(left8, 0.0, high), jnp.where(left8, 0.0, low)], axis=0),
-                ],
-                axis=0,
-            ).astype(BF16)
-            blank = jnp.zeros((32, 128), BF16)
-            lines.append(
-                jnp.concatenate([blank, feats] if u % 2 else [feats, blank], axis=1)
-            )
-            if u % 2:
-                got = lax.dot_general(
-                    jnp.concatenate(lines, axis=0),
-                    jnp.concatenate([weights[u - 1], weights[u]], axis=1),
-                    (((1,), (1,)), ((), ())),
-                    preferred_element_type=F32,
+        outs = []
+        for u in range(0, UNROLL, 2):
+            rolled = [pltpu.roll(tile, 64, 1) for tile in tiles[u : u + 2]]
+            for side in range(2):
+                lines = []
+                for tile, turn in zip(tiles[u : u + 2], rolled):
+                    twice = jnp.where(left8, turn, tile) if side else jnp.where(left8, tile, turn)
+                    high = twice.astype(BF16).astype(F32)
+                    lines.append(jnp.concatenate([high, twice - high], axis=0).astype(BF16))
+                outs.append(
+                    jnp.dot(
+                        jnp.concatenate(lines, axis=0),
+                        weights[u + side],
+                        preferred_element_type=F32,
+                    )
                 )
-                outs += [got[0:32], got[32:64]]
-                lines = []
-        for u in range(UNROLL):
-            ca, cb = ids[u]
-            got = outs[u]
-            acc_ref[ca] = acc_ref[ca] + (got[0:8] + got[8:16])
-            acc_ref[cb] = acc_ref[cb] + (got[16:24] + got[24:32])
+        for u in range(0, UNROLL, 2):
+            for side in range(2):
+                got = outs[u + side]
+                for n in range(2):
+                    cell = ids[u + n][side]
+                    acc_ref[n, cell] = acc_ref[n, cell] + (
+                        got[16 * n : 16 * n + 8] + got[16 * n + 8 : 16 * n + 16]
+                    )
         return carry
 
     lax.fori_loop(0, (live + UNROLL - 1) // UNROLL, block, 0)
 
     def finish(a, carry):
         for p in range(PAIRS):
-            ta = acc_ref[a * CB + 2 * p]
-            tb = acc_ref[a * CB + 2 * p + 1]
-            total = jnp.where(left8, ta + pltpu.roll(ta, 64, 1), tb + pltpu.roll(tb, 64, 1))
+            one, two = a * CB + 2 * p, a * CB + 2 * p + 1
+            total = jnp.where(
+                left8,
+                acc_ref[0, one] + pltpu.roll(acc_ref[1, one], 64, 1),
+                pltpu.roll(acc_ref[0, two], 64, 1) + acc_ref[1, two],
+            )
             tile = rec_ref[a, p]
             near = near_ref[a, p]
             h, sound = tile[10:11], tile[12:13]
@@ -762,16 +760,14 @@
             jax.ShapeDtypeStruct((CA, CB, 256), F32),
             jax.ShapeDtypeStruct((CA, PAIRS, 128), F32),
         ),
-        in_specs=[pl.BlockSpec(memory_space=pltpu.VMEM)] * 3
-        + [pl.BlockSpec(memory_space=pl.ANY)],
+        in_specs=[pl.BlockSpec(memory_space=pltpu.VMEM)] * 4,
         out_specs=[pl.BlockSpec(memory_space=pltpu.VMEM)] * 2,
         scratch_shapes=[
-            pltpu.VMEM((CA * CB, 64, 128), BF16),
-            pltpu.VMEM((CA * CB, 8, 128), F32),
-            pltpu.VMEM((recv.shape[0], 128), jnp.int32),
-            pltpu.SMEM((recv.shape[0], 128), jnp.int32),
+            pltpu.VMEM((2, CA * CB, 8, 128), F32),
+            pltpu.VMEM((16, recv.shape[0]), jnp.int32),
+            pltpu.SMEM((16, recv.shape[0]), jnp.int32),
             pltpu.SMEM((recv.shape[0] * SLOTS // 2 + UNROLL + 8,), jnp.int32),
-            pltpu.SemaphoreType.DMA((2,)),
+            pltpu.SemaphoreType.DMA((1,)),
         ],
         compiler_params=pltpu.CompilerParams(vmem_limit_bytes=10 << 20),
         name="wall_terms",

time: 81.9 us -> 77.4 us (0.945)
  the two profiles are of different devices: /device:TPU:0 before, /device:TPU:40 now
where the time goes in v6:
time: 77.4 us; the launch traced here: 76.4 us
  Pallas kernels  74.4 us (96%)
  local copies, waits for them, and re-layouts  1.3 us (2%)
    pallas_call x1, Pallas kernels, near_and_exchange(): pl.pallas_call(lambda *refs: exchange_kernel(devices, *refs), out_shape=(...  52.7 us
    pallas_call x1, Pallas kernels, wall_terms(): pl.pallas_call(wall_kernel, out_shape=(jax.ShapeDtypeStruct((CA, CB, 256)...  21.7 us

profile of v6, /device:TPU:40, one launch (start us, length us, event | category | flops | bytes accessed | tf_op | source)
XLA Modules:
  0.0 76.4 jit_solution(1522129637190425801)
XLA Ops:
  0.6 0.0 copy-start
  0.6 0.7 copy-done
  1.3 52.7 %near_and_exchange.1 = (f32[16,4,8,128]{3,2,1,0:T(8,128)S(1)}, f32[16,4,16,128]{3,2,1,0:T(8,128)S(1)}, bf16[128,2,64,128]{3,2,1,0:T(8,128)(2,1)S(1)}, f32[128,40,128]{2,1,0:T(8,128)S(1)}) custom-call(s32[8,16]{1,0:T(8,128)S(1)} %bitcast.8, f32[16,8,768]{2,1,0:T(8,128)} %refs_1_.1, f32[256,512]{1,0:T(8,128)} %refs_2_.1, s32[2,256]{1,0:T(2,128)} %bitcast.10, ...), custom_call_target="tpu_custom_call" | custom-call | tf_op jit(solution)/shard_map/near_and_exchange/pallas_call | solution.py:566
  54.1 21.7 %wall_terms.1 = (f32[16,8,256]{2,1,0:T(8,128)}, f32[16,4,128]{2,1,0:T(4,128)S(1)}) custom-call(f32[128,40,128]{2,1,0:T(8,128)S(1)} %get-tuple-element.8.recv_ref, f32[16,4,16,128]{3,2,1,0:T(8,128)S(1)} %get-tuple-element.9.rec_ref, f32[16,4,8,128]{3,2,1,0:T(8,128)S(1)} %get-tuple-element.10.near_ref, bf16[128,2,64,128]{3,2,1,0:T(8,128)(2,1)S(1)} %get-tuple-element.11.side_ref), custom_call_target="tpu_custom_call" | custom-call | tf_op jit(solution)/shard_map/wall_terms/pallas_call | solution.py:757
  75.8 0.6 copy.9
Async XLA Ops:
  0.6 0.7 copy-start

commit v7 on v6

--- a/solution.py
+++ b/solution.py
@@ -155,7 +155,7 @@
 
 
 def near_compute(
-    post, settle, ext_ref, out_ref, side_out, feat_ref, turn_ref, side_ref, geo_ref, sd0, mid0, mix0, sd1, mid1, mix1
+    post, settle, ext_ref, out_ref, side_out, mean_ref, feat_ref, turn_ref, side_ref, geo_ref, sd0, mid0, mix0, sd1, mid1, mix1
 ):
     left1 = iota((1, 128), 1) < 64
     left8 = iota((8, 128), 1) < 64
@@ -164,14 +164,20 @@
     zero8 = jnp.zeros((8, 128), F32)
     zero16 = jnp.zeros((16, 128), BF16)
     own = jnp.where(left1, -1.0, 0.0)
+    for n, c in enumerate((3, 4, 5, 11)):
+        mean_ref[n : n + 1, :] = jnp.broadcast_to(
+            jnp.mean(ext_ref[CA // 2, 2, c : c + 1, :], axis=1, keepdims=True), (1, 128)
+        )
+    mean = {c: mean_ref.at[n : n + 1, :] for n, c in enumerate((3, 4, 5, 11))}
 
     def prepare(a, p):
         row = lambda c: ext_ref[a, p, c : c + 1, :]
+        level = lambda c: row(c) - mean[c][...]
         x = row(0) - 0.5
         y = row(1) + own
         z = row(2) - 2.0
-        u, v, w, mass = row(3), row(4), row(5), row(6) * (-32.0 * KERN_F)
-        pres, visc, inv, h, heat = row(7), row(8), row(9), row(10), row(11)
+        u, v, w, mass = level(3), level(4), level(5), row(6) * (-32.0 * KERN_F)
+        pres, visc, inv, h, heat = row(7), row(8), row(9), row(10), level(11)
         one = jnp.ones_like(x)
         head = [one, pres, u, one, pres, v]
         v0 = mass * stack_rows(row8, head + [w, z])
@@ -347,7 +353,7 @@
         geo = lambda c: geo_ref[a + 1, p + 1, c : c + 1, :]
         x, y, z = geo(0), geo(1), geo(2)
         row = lambda c: ext_ref[a + 1, p + 1, c : c + 1, :]
-        u, v, w = row(3), row(4), row(5)
+        u, v, w = [row(c) - mean[c][...] for c in (3, 4, 5)]
         sm, smp = v0[0:1], v0[1:2]
         gx = x * sm - v1[0:1]
         gy = y * sm - v1[3:4]
@@ -368,7 +374,7 @@
         ax = ax - (pi * gx + (x * smp - v1[1:2]))
         ay = ay - (pi * gy + (y * smp - v1[4:5]))
         az = az - (pi * gz + (z * smp - v1[6:7]))
-        heat = (2.0 * KAPPA) * inv * (row(11) * smi - v2[4:5])
+        heat = (2.0 * KAPPA) * inv * ((row(11) - mean[11][...]) * smi - v2[4:5])
         for n, line in enumerate((density, ax, ay, az, heat)):
             out_ref[a, p, n : n + 1, :] = line
 
@@ -404,12 +410,12 @@
             k = 2 * m + odd
             sd_ref, mid_ref, mix_ref = slots[odd]
             sd_next, mid_last, mix_last = slots[1 - odd]
+            post(CA * SENDS + k * STEP_SENDS + 1)
             gather(jnp.clip(k - 1, 0, last), mid_last, mix_last)
             distances(jnp.minimum(k + 1, last), sd_next)
             weigh(sd_ref, mid_ref, mix_ref)
             wall_side(jnp.minimum(k, last))
-            for n in range(STEP_SENDS):
-                post(CA * SENDS + k * STEP_SENDS + n + 1)
+            post(CA * SENDS + k * STEP_SENDS + 2)
         return carry
 
     lax.fori_loop(0, CA * PAIRS // 2, step, 0)
@@ -418,7 +424,7 @@
 
 def exchange_kernel(
     devices,
-    counts_ref,
+    counts_hbm,
     fluid_hbm,
     wall_hbm,
     readers_hbm,
@@ -427,6 +433,7 @@
     rec_ref,
     side_out,
     recv_ref,
+    counts_ref,
     fluid_ref,
     wall_ref,
     readers_ref,
@@ -449,6 +456,7 @@
                 (targets_hbm, targets_ref),
                 (wall_hbm, wall_ref),
                 (fluid_hbm, fluid_ref),
+                (counts_hbm, counts_ref),
             ]
         )
     ]
@@ -491,6 +499,7 @@
             ext_ref[a, PAIRS + 1] = blank
 
     loads[3].wait()
+    loads[4].wait()
     pack_records(counts_ref, fluid_ref, rec_ref, greet)
     for load in loads[:3]:
         load.wait()
@@ -571,9 +580,10 @@
             jax.ShapeDtypeStruct((CA * CB, 2, 64, 128), BF16),
             jax.ShapeDtypeStruct((devices, 40, 128), F32),
         ),
-        in_specs=[pl.BlockSpec(memory_space=pltpu.SMEM)] + [hbm] * 4,
+        in_specs=[hbm] * 5,
         out_specs=[vmem, vmem, vmem, anywhere],
         scratch_shapes=[
+            pltpu.SMEM(counts_t.shape, jnp.int32),
             pltpu.VMEM(fluid_state.shape, F32),
             pltpu.VMEM(wall_blocks.shape, F32),
             pltpu.VMEM(readers_t.shape, jnp.int32),
@@ -582,6 +592,7 @@
             pltpu.VMEM((devices * SLOTS // 2, 2 * walls), BF16),
             pltpu.VMEM((2 * walls, 384), BF16),
             pltpu.VMEM((18, 6, 16, 128), F32),
+            pltpu.VMEM((8, 128), F32),
             pltpu.VMEM((18, 6, 3, 64, 128), BF16),
             pltpu.VMEM((18, 6, 128, 128), BF16),
             pltpu.VMEM((18, PAIRS, 64, 128), BF16),
@@ -594,7 +605,7 @@
         ]
         * 2
         + [
-            pltpu.SemaphoreType.DMA((4,)),
+            pltpu.SemaphoreType.DMA((5,)),
             pltpu.SemaphoreType.DMA,
             pltpu.SemaphoreType.DMA,
             pltpu.SemaphoreType.DMA,
@@ -606,10 +617,9 @@
         ),
         name="near_and_exchange",
     )(
-        counts_t,
         *[
             pltpu.with_memory_space_constraint(array, pltpu.HBM)
-            for array in (fluid_state, wall_blocks, readers_t, targets_t)
+            for array in (counts_t, fluid_state, wall_blocks, readers_t, targets_t)
         ],
     )
 

time: 77.4 us -> 75.7 us (0.978)
  the two profiles are of different devices: /device:TPU:40 before, /device:TPU:25 now
where the time goes in v7:
time: 75.7 us; the launch traced here: 75.5 us
  Pallas kernels  74.3 us (98%)
    pallas_call x1, Pallas kernels, near_and_exchange(): pl.pallas_call(lambda *refs: exchange_kernel(devices, *refs), out_shape=(...  52.6 us
    pallas_call x1, Pallas kernels, wall_terms(): pl.pallas_call(wall_kernel, out_shape=(jax.ShapeDtypeStruct((CA, CB, 256)...  21.6 us

profile of v7, /device:TPU:25, one launch (start us, length us, event | category | flops | bytes accessed | tf_op | source)
XLA Modules:
  0.0 75.5 jit_solution(4989656712803531544)
XLA Ops:
  0.6 52.6 %near_and_exchange.1 = (f32[16,4,8,128]{3,2,1,0:T(8,128)S(1)}, f32[16,4,16,128]{3,2,1,0:T(8,128)S(1)}, bf16[128,2,64,128]{3,2,1,0:T(8,128)(2,1)S(1)}, f32[128,40,128]{2,1,0:T(8,128)S(1)}) custom-call(s32[8,16]{1,0:T(8,128)} %bitcast.9, f32[16,8,768]{2,1,0:T(8,128)} %refs_1_.1, f32[256,512]{1,0:T(8,128)} %refs_2_.1, s32[2,256]{1,0:T(2,128)} %bitcast.10, ...), custom_call_target="tpu_custom_call" | custom-call | tf_op jit(solution)/shard_map/near_and_exchange/pallas_call | solution.py:575
  53.3 21.6 %wall_terms.1 = (f32[16,8,256]{2,1,0:T(8,128)}, f32[16,4,128]{2,1,0:T(4,128)S(1)}) custom-call(f32[128,40,128]{2,1,0:T(8,128)S(1)} %get-tuple-element.8.recv_ref, f32[16,4,16,128]{3,2,1,0:T(8,128)S(1)} %get-tuple-element.9.rec_ref, f32[16,4,8,128]{3,2,1,0:T(8,128)S(1)} %get-tuple-element.10.near_ref, bf16[128,2,64,128]{3,2,1,0:T(8,128)(2,1)S(1)} %get-tuple-element.11.side_ref), custom_call_target="tpu_custom_call" | custom-call | tf_op jit(solution)/shard_map/wall_terms/pallas_call | solution.py:767
  74.9 0.6 copy.9
